TPU v7x, 32 devices: a whole 2x2x4 slice. The times are simulated.
32 devices in a mesh: dom: 8 (over z, x), rep: 4 (over y, core).
Axes of the slice: x: 2, y: 2, z: 4, core: 2. Of those that a mesh axis runs over, the one named last changes fastest.
Arguments:
- features: bfloat16 [2048, 256], P('dom'), may hold values from -6 to 6
- positions: float32 [3, 2048], P(None, 'dom'), may hold values from -6 to 6
- radial: bfloat16 [8, 256, 256], replicated, may hold values from -0.03125 to 0.03125
- mixing: bfloat16 [256, 256], replicated, may hold values from -0.375 to 0.375
- readout: float32 [256], replicated, may hold values from -4 to 4
- decay: float32 [8], replicated, may hold values from 0.1 to 1
- send_rows: int32 [4, 1024], P(None, 'dom'), may hold values from 0 to 255
- pair_home: int32 [1536], P(('dom', 'rep')), may hold values from 0 to 1
- pair_other: int32 [1536], P(('dom', 'rep')), may hold values from 0 to 5
- pair_kind: int32 [1536], P(('dom', 'rep')), may hold values from 0 to 7
- pair_image: int32 [3, 1536], P(None, ('dom', 'rep')), may hold values from -1 to 1
Outputs:
- grad_features: bfloat16 [2048, 256], P('dom')
- forces: float32 [3, 2048], P(None, 'dom')
- virials: float32 [6, 2048], P(None, 'dom')
- grad_mixing: float32 [256, 256], P('dom', 'rep')
Inputs may be any that keep to these rules, and one draw needn't show every extreme that they name: `send_rows`: rows may repeat within a round.
All inputs are finite; a program needn't handle non-finite values.
Results may differ from a plain program's by a relative error of at most 0.006.
Values may be sent and summed in bfloat16 or wider, within the bound.
A program may use at most 128 MiB of HBM per device.

v0:
```python
import functools

import jax
import jax.numpy as jnp
from jax import lax
from jax.experimental import pallas as pl
from jax.experimental.pallas import tpu as pltpu
from jax.sharding import PartitionSpec as P

TILE = 128
OFFSETS = (1, -1, 2, -2)
CELL = 2.0
GROUP = 4
BACK_GROUP = 12
WIDE = 8
F32 = jnp.float32
BF16 = jnp.bfloat16
MESH = pl.DeviceIdType.MESH
VMEM = pl.BlockSpec(memory_space=pltpu.VMEM)
HBM = pl.BlockSpec(memory_space=pltpu.HBM)


def nt(a, b):
    return lax.dot_general(a, b, (((1,), (1,)), ((), ())), preferred_element_type=F32)


def tn(a, b):
    return lax.dot_general(a, b, (((0,), (0,)), ((), ())), preferred_element_type=F32)


def mm(a, b):
    return jnp.dot(a, b, preferred_element_type=F32)


def split3(x):
    hi = x.astype(BF16)
    rest = x - hi.astype(F32)
    mid = rest.astype(BF16)
    low = (rest - mid.astype(F32)).astype(BF16)
    return hi, mid, low


def front_kernel(n_dom, n_rep, feat_h, pos_h, rows_h, radial_h, mixing_h, readout_h, decay_h, home_h, other_h,
                 kind_h, image_h, mapped, tiles, kern_t, packed, slope, adjoint, radial,
                 feat, pos, rows, mixing, readout, decay, home, other, kind, image,
                 sendf, sendp, recvf, recvp, col, kern_f, acc, msg, recv, pk, sl,
                 load, sf, sp, rf, rp, s4, r4, s5, r5, s1, r1, s2, r2, s3, r3):
    d = lax.axis_index("dom")
    r = lax.axis_index("rep")
    loads = [pltpu.make_async_copy(src, dst, load.at[i]) for i, (src, dst) in enumerate((
        (rows_h, rows), (feat_h, feat), (pos_h, pos), (radial_h, radial), (decay_h, decay), (home_h, home),
        (other_h, other), (kind_h, kind), (image_h, image), (mixing_h, mixing), (readout_h, readout)))]
    for copy in loads:
        copy.start()
    barrier = pltpu.get_barrier_semaphore()
    c = lax.rem(r, 2)
    partner = {"dom": d, "rep": r + 1 - 2 * c}
    steps = (c + 1, -(c + 1))
    for o in steps:
        pl.semaphore_signal(barrier, inc=1, device_id={"dom": lax.rem(d + o + n_dom, n_dom), "rep": r},
                            device_id_type=MESH)
    peers = [lax.rem(r + i, n_rep) for i in range(1, n_rep)]
    for q in peers:
        pl.semaphore_signal(barrier, inc=1, device_id={"dom": d, "rep": q}, device_id_type=MESH)
    atoms = feat.shape[0]
    own = atoms // TILE
    iota = lax.broadcasted_iota(jnp.int32, (atoms, TILE), 0)
    for copy in loads[:3]:
        copy.wait()
    copies = []
    hots = []
    for q in range(2):
        hot = (iota == rows[pl.ds(2 * c + q, 1), :]).astype(F32)
        hots.append(hot.astype(BF16))
        sendp[q] = jnp.dot(pos[...], hot, precision=lax.Precision.HIGHEST, preferred_element_type=F32)
    pl.semaphore_wait(barrier, 2 + n_rep - 1)
    targets = [{"dom": lax.rem(d + o + n_dom, n_dom), "rep": r} for o in steps]
    for src, dst, ss, rs in ((sendp, recvp, sp, rp), (sendf, recvf, sf, rf)):
        for q in range(2):
            t = 2 * c + q
            if src is sendf:
                sendf[q] = tn(hots[q], feat[...]).astype(BF16)
            copies.append(pltpu.make_async_remote_copy(src.at[q], dst.at[t], ss.at[q], rs.at[t],
                                                       device_id=targets[q], device_id_type=MESH))
            copies[-1].start()

    def columns(j):
        for c in range(3):
            col[j, c] = jnp.transpose(jnp.broadcast_to(tiles[j][c:c + 1, :], (TILE, TILE)))

    for copy in loads[3:]:
        copy.wait()
    for j in range(own):
        tiles[j] = pos[:, j * TILE:(j + 1) * TILE]
        columns(j)

    def local(k, _):
        res = mm(feat[...], radial[k]).astype(BF16)
        for j in range(own):
            mapped[j, k] = res[j * TILE:(j + 1) * TILE]
        return 0

    lax.fori_loop(0, radial.shape[0], local, 0)
    def distant(base, k):
        both = recvf[pl.ds(base, 2)].reshape(2 * TILE, -1)
        res = mm(both, radial[k]).astype(BF16)
        mapped[own + base, k] = res[:TILE]
        mapped[own + base + 1, k] = res[TILE:]

    def spread(base):
        lax.fori_loop(0, radial.shape[0], lambda k, _: (distant(base, k), 0)[1], 0)

    relays = []

    def relay(buf, first, ss, rs):
        for q in range(2):
            t = 2 * c + q
            copies[first + q].wait_recv()
            relays.append(pltpu.make_async_remote_copy(buf.at[t], buf.at[t], ss.at[q], rs.at[t],
                                                       device_id=partner, device_id_type=MESH))
            relays[-1].start()

    def relayed(buf, ss, rs):
        for q in range(2):
            t = 2 * (1 - c) + q
            pltpu.make_async_remote_copy(buf.at[t], buf.at[t], ss.at[q], rs.at[t],
                                         device_id=partner, device_id_type=MESH).wait_recv()

    pairs = home.shape[0]
    steps_all = pairs // GROUP

    def kernels(g, _):
        for u in range(GROUP):
            p = g * GROUP + u
            h, o, k = home[p], other[p], kind[p]
            row = tiles[o]
            d2 = None
            for x in range(3):
                sep = (row[x:x + 1, :] + image[x, p].astype(F32) * CELL) - col[h, x]
                d2 = sep * sep if d2 is None else d2 + sep * sep
            kern = jnp.exp(d2 * (-decay[k]))
            for i in range(own):
                kern_f[p, i * TILE:(i + 1) * TILE, :] = (kern * (h == i).astype(F32)).astype(BF16)
        return 0

    relay(recvp, 0, s5, r5)
    relayed(recvp, s5, r5)
    for t in range(4):
        tiles[own + t] = recvp[t]
        columns(own + t)
    lax.fori_loop(0, steps_all // 2, kernels, 0)
    relay(recvf, 2, s4, r4)
    lax.fori_loop(steps_all // 2, steps_all, kernels, 0)
    spread(2 * c)
    relayed(recvf, s4, r4)
    spread(2 * (1 - c))

    acc[...] = jnp.zeros_like(acc)

    def forward(g, _):
        left = [kern_f[g * WIDE + u] for u in range(WIDE)]
        right = [mapped[other[g * WIDE + u], kind[g * WIDE + u]] for u in range(WIDE)]
        acc[...] += mm(jnp.concatenate(left, axis=1), jnp.concatenate(right, axis=0))
        return 0

    lax.fori_loop(0, pairs // WIDE, forward, 0)
    share = atoms // n_rep
    for q in range(n_rep):
        msg[q] = acc[q * share:(q + 1) * share, :].astype(BF16)

    def push(src, dst, ss, rs, q):
        copy = pltpu.make_async_remote_copy(src, dst, ss, rs, device_id={"dom": d, "rep": q},
                                            device_id_type=MESH)
        copy.start()
        return copy

    def take(dst, ss, rs, q):
        pltpu.make_async_remote_copy(dst, dst, ss, rs, device_id={"dom": d, "rep": q},
                                     device_id_type=MESH).wait_recv()

    def transposed(g, _):
        for u in range(GROUP):
            p = g * GROUP + u
            h, o, k = home[p], other[p], kind[p]
            row = tiles[h]
            d2 = None
            for c in range(3):
                sep = col[o, c] - (row[c:c + 1, :] - image[c, p].astype(F32) * CELL)
                d2 = sep * sep if d2 is None else d2 + sep * sep
            kern_t[p] = jnp.exp(d2 * (-decay[k]))
        return 0

    sent = [push(msg.at[q], recv.at[r], s1.at[i], r1.at[r], q) for i, q in enumerate(peers)]
    half = pairs // GROUP // 2
    lax.fori_loop(0, half, transposed, 0)
    total = msg[r].astype(F32)
    for i, q in enumerate(peers):
        take(recv.at[q], s1.at[i], r1.at[q], q)
        total = total + recv[q].astype(F32)
    low = total.astype(BF16)
    pk[r] = low
    mixed = mm(low, mixing[...])
    sig = jax.nn.sigmoid(mixed)
    sl[r] = (readout[...] * sig * (1.0 + mixed * (1.0 - sig))).astype(BF16)
    sent += [push(sl.at[r], sl.at[r], s3.at[i], r3.at[r], q) for i, q in enumerate(peers)]
    sent += [push(pk.at[r], pk.at[r], s2.at[i], r2.at[r], q) for i, q in enumerate(peers)]
    lax.fori_loop(half, pairs // GROUP, transposed, 0)
    for i, q in enumerate(peers):
        take(sl.at[q], s3.at[i], r3.at[q], q)
    full = sl[...].reshape(-1, mixing.shape[0])
    slope[...] = full
    adj = nt(full, mixing[...]).astype(BF16)
    for j in range(own):
        adjoint[j] = adj[j * TILE:(j + 1) * TILE]
    for i, q in enumerate(peers):
        take(pk.at[q], s2.at[i], r2.at[q], q)
    packed[...] = pk[...].reshape(-1, mixing.shape[0])
    for copy in copies + relays + sent:
        copy.wait_send()


def backward_kernel(n_rep, decay_h, home_h, other_h, kind_h, image_h, tiles, mapped, kern_t, adjoint, radial,
                    packed, slope, gfeat, side, mix, decay, home, other, kind, image, moments, first, second,
                    acc, load):
    loads = [pltpu.make_async_copy(src, dst, load.at[i]) for i, (src, dst) in enumerate((
        (decay_h, decay), (home_h, home), (other_h, other), (kind_h, kind), (image_h, image)))]
    for copy in loads:
        copy.start()
    n_ext = tiles.shape[0]
    for j in range(n_ext):
        pos = tiles[j]
        x, y, z = pos[0:1, :], pos[1:2, :], pos[2:3, :]
        zero = jnp.zeros((2, TILE), F32)
        one_rows = jnp.concatenate([x, y, z, x, x, y, zero], axis=0)
        two_rows = jnp.concatenate([x, y, z, y, z, z, zero], axis=0)
        first[j] = one_rows
        second[j] = two_rows
        stack = jnp.concatenate([one_rows * two_rows, one_rows, two_rows], axis=0)
        parts = [v.astype(F32) for v in split3(stack)]
        table = jnp.concatenate(
            [parts[0], jnp.ones((8, TILE), F32), parts[1], parts[2]], axis=0).astype(BF16)
        moments[j] = jnp.concatenate([table, table], axis=1)
    acc[...] = jnp.zeros_like(acc)
    side[...] = jnp.zeros_like(side)
    sub = lax.broadcasted_iota(jnp.int32, (8, TILE), 0)

    def rows_of(a, b):
        return ((sub == a[0]) | (sub == a[1]) | (sub == a[2])), ((sub == b[0]) | (sub == b[1]))

    is_x1, is_y1 = rows_of((0, 3, 4), (1, 5))
    is_x2, is_y2 = (sub == 0), ((sub == 1) | (sub == 3))

    def fold(res):
        quad = res[0:8] + res[32:40] + res[56:64]
        lin1 = res[8:16] + res[40:48] + res[64:72]
        lin2 = res[16:24] + res[48:56] + res[72:80]
        return quad, lin1, lin2, res[24:32]

    def combine(res, a, b):
        quad, lin1, lin2, one = fold(res)
        force = lin1 - a * one
        virial = -0.5 * (quad - a * lin2 - b * lin1 + a * b * one)
        return jnp.concatenate([force, virial], axis=0)

    for copy in loads:
        copy.wait()

    def body(g, _):
        found = []
        names = []
        weights = []
        for u in range(BACK_GROUP):
            p = g * BACK_GROUP + u
            h, o, k = home[p], other[p], kind[p]
            names.append((p, h, o, k))
            kern = kern_t[p]
            weight = (-2.0 * decay[k]) * kern * nt(mapped[o, k], adjoint[h])
            hi = weight.astype(BF16)
            lo = (weight - hi.astype(F32)).astype(BF16)
            weights.append((hi, lo))
        for (p, h, o, k), (hi, lo) in zip(names, weights):
            back = mm(kern_t[p].astype(BF16), adjoint[h]).astype(BF16)
            part = nt(back, radial[k])
            shift = [image[c, p].astype(F32) * CELL for c in range(3)]
            near_res = mm(moments[o], jnp.concatenate([hi, lo], axis=0))
            far_res = nt(moments[h], jnp.concatenate([hi, lo], axis=1))
            s1 = jnp.where(is_x1, shift[0], jnp.where(is_y1, shift[1], shift[2]))
            s2 = jnp.where(is_x2, shift[0], jnp.where(is_y2, shift[1], shift[2]))
            near_side = combine(near_res, first[h] - s1, second[h] - s2)
            far_side = combine(far_res, first[o] + s1, second[o] + s2)
            found.append((h, o, part, near_side, far_side))
        for h, o, part, near_side, far_side in found:
            acc[o] += part
            side[h] += near_side
            side[o] += far_side
        return 0

    lax.fori_loop(0, home.shape[0] // BACK_GROUP, body, 0)
    for j in range(n_ext):
        for half in range(2):
            gfeat[j, half] = acc[j, :, half * TILE:(half + 1) * TILE].astype(BF16)
    r = lax.axis_index("rep")
    channels = slope.shape[1]
    share = channels // n_rep
    pick = (lax.broadcasted_iota(jnp.int32, (channels, share), 0)
            == lax.broadcasted_iota(jnp.int32, (channels, share), 1) + r * share).astype(BF16)
    cols = mm(slope[...], pick).astype(BF16)
    res = tn(packed[...], cols)
    mix[...] = res.reshape(mix.shape)


def return_kernel(n_dom, n_rep, gfeat, side, mix, rows, out_feat, out_force, out_virial, out_mix,
                  gp, gs, sb, ss, rf, rs, rm, part, pside, qside,
                  sem_gf, sem_hf, sem_gs, sem_hs, sem_sf, sem_rf, sem_ss, sem_rs, sem_sm, sem_rm, sem_sp, sem_rp, sem_sq, sem_rq):
    d = lax.axis_index("dom")
    r = lax.axis_index("rep")
    y = lax.div(r, 2)
    c = lax.rem(r, 2)

    def dom_at(o):
        return lax.rem(d + o + n_dom, n_dom)

    barrier = pltpu.get_barrier_semaphore()

    def hello(dom, rep):
        pl.semaphore_signal(barrier, inc=1, device_id={"dom": dom, "rep": rep}, device_id_type=MESH)

    mine = [(c + 1), -(c + 1)]
    peers = [lax.rem(r + i, n_rep) for i in range(1, n_rep)]
    for o in mine:
        for half in range(n_rep // 2):
            hello(dom_at(o), 2 * half + c)
    for q in peers:
        hello(d, q)

    def greet(i, _):
        hello(lax.rem(d + i, n_dom), r)
        return 0

    lax.fori_loop(1, n_dom, greet, 0)
    pl.semaphore_wait(barrier, n_rep + n_rep - 1 + n_dom - 1)

    partner = {"dom": d, "rep": r + 1 - 2 * c}
    mate = 1 - c
    sends = []
    swaps = []
    for slot, j in ((1, 2 + 2 * mate), (2, 3 + 2 * mate), (0, mate)):
        cf = pltpu.make_async_remote_copy(gfeat.at[j], gp.at[slot], sem_gf.at[slot], sem_hf.at[slot],
                                          device_id=partner, device_id_type=MESH)
        cs = pltpu.make_async_remote_copy(side.at[j], gs.at[slot], sem_gs.at[slot], sem_hs.at[slot],
                                          device_id=partner, device_id_type=MESH)
        cf.start()
        cs.start()
        swaps.append((cf, cs))
        sends += [cf, cs]
    for (cf, cs), (slot, j) in zip(swaps, ((1, 2 + 2 * c), (2, 3 + 2 * c), (0, c))):
        cf.wait_recv()
        cs.wait_recv()
        sb[slot] = (gfeat[j].astype(F32) + gp[slot].astype(F32)).astype(BF16)
        ss[slot] = side[j] + gs[slot]
        for half in ((0, 1) if slot else (1 - y,)):
            dest = {"dom": dom_at(-mine[slot - 1]) if slot else d, "rep": 2 * half + c}
            nf = pltpu.make_async_remote_copy(sb.at[slot, half], rf.at[slot, y], sem_sf.at[slot, half],
                                              sem_rf.at[slot, y], device_id=dest, device_id_type=MESH)
            ns = pltpu.make_async_remote_copy(ss.at[slot], rs.at[slot, y], sem_ss.at[slot, half],
                                              sem_rs.at[slot, y], device_id=dest, device_id_type=MESH)
            nf.start()
            ns.start()
            sends += [nf, ns]

    def mix_copy(i):
        to = lax.rem(d + i, n_dom)
        return pltpu.make_async_remote_copy(mix.at[to], rm.at[d], sem_sm.at[i], sem_rm.at[d],
                                            device_id={"dom": to, "rep": r}, device_id_type=MESH)

    def mix_start(i, _):
        mix_copy(i).start()
        return 0

    lax.fori_loop(1, n_dom, mix_start, 0)

    def take(dst, ss, rsem):
        pltpu.make_async_remote_copy(dst, dst, ss, rsem, device_id={"dom": d, "rep": peers[0]},
                                     device_id_type=MESH).wait_recv()

    take(rf.at[0, 1 - y], sem_sf.at[0, 0], sem_rf.at[0, 1 - y])
    take(rs.at[0, 1 - y], sem_ss.at[0, 0], sem_rs.at[0, 1 - y])
    feat_self = sb[0, y].astype(F32) + rf[0, 1 - y].astype(F32)
    side_self = ss[0] + rs[0, 1 - y]
    is_low = c == 0
    zero = jnp.zeros_like(feat_self)
    total = jnp.concatenate([jnp.where(is_low, feat_self, zero), jnp.where(is_low, zero, feat_self)], axis=0)
    zside = jnp.zeros_like(side_self)
    total_side = jnp.concatenate([jnp.where(is_low, side_self, zside), jnp.where(is_low, zside, side_self)],
                                 axis=1)
    atoms = out_feat.shape[0]
    iota = lax.broadcasted_iota(jnp.int32, (atoms, TILE), 0)
    for q in range(2):
        hot = (iota == rows[pl.ds(2 * c + q, 1), :]).astype(F32).astype(BF16)
        slot = 1 + q
        got = None
        for s in range(n_rep // 2):
            take(rf.at[slot, s], sem_sf.at[0, 0], sem_rf.at[slot, s])
            take(rs.at[slot, s], sem_ss.at[0, 0], sem_rs.at[slot, s])
            total = total + mm(hot, rf[slot, s])
            got = rs[slot, s] if got is None else got + rs[slot, s]
        for v in split3(got):
            total_side = total_side + nt(v, hot)
    part[r] = total.astype(BF16)
    pside[...] = total_side
    phase = []
    for i, q in enumerate(peers):
        cp = pltpu.make_async_remote_copy(part.at[r], part.at[r], sem_sp.at[i], sem_rp.at[r],
                                          device_id={"dom": d, "rep": q}, device_id_type=MESH)
        cp.start()
        phase.append(cp)
    cq = pltpu.make_async_remote_copy(pside, qside, sem_sq, sem_rq,
                                      device_id={"dom": d, "rep": r + 1 - 2 * c}, device_id_type=MESH)
    cq.start()

    def mix_add(i, value):
        frm = lax.rem(d + i, n_dom)
        take(rm.at[frm], sem_sm.at[0], sem_rm.at[frm])
        return value + rm[frm]

    out_mix[...] = lax.fori_loop(1, n_dom, mix_add, mix[d])
    cq.wait_recv()
    final = total_side + qside[...]
    out_force[...] = final[0:3]
    out_virial[...] = final[8:14]
    for q in peers:
        take(part.at[q], sem_sp.at[0], sem_rp.at[q])
    for half in range(2):
        out_feat[:, half * TILE:(half + 1) * TILE] = (
            part[2 * half].astype(F32) + part[2 * half + 1].astype(F32)).astype(BF16)
    for copy in sends:
        copy.wait_send()

    def mix_done(i, _):
        mix_copy(i).wait_send()
        return 0

    lax.fori_loop(1, n_dom, mix_done, 0)
    for cp in phase:
        cp.wait_send()
    cq.wait_send()


def copy_out(a, b, c, d, a_h, b_h, c_h, d_h, sem):
    copies = [pltpu.make_async_copy(src, dst, sem.at[i])
              for i, (src, dst) in enumerate(((a, a_h), (b, b_h), (c, c_h), (d, d_h)))]
    for copy in copies:
        copy.start()
    for copy in copies:
        copy.wait()


def on_device(n_dom, n_rep, features, positions, radial, mixing, readout, decay, send_rows, pair_home,
              pair_other, pair_kind, pair_image):
    atoms, channels = features.shape
    own = atoms // TILE
    n_ext = own + len(OFFSETS)
    kinds = radial.shape[0]
    dma = pltpu.SemaphoreType.DMA
    share = atoms // n_rep

    def params(cid=None):
        if cid is None:
            return pltpu.CompilerParams(vmem_limit_bytes=40 << 20)
        return pltpu.CompilerParams(collective_id=cid, has_side_effects=True, vmem_limit_bytes=40 << 20)

    def shape(dims, dtype):
        return jax.ShapeDtypeStruct(dims, dtype)

    def pair_tables():
        return [pltpu.SMEM(decay.shape, F32)] + [
            pltpu.SMEM(a.shape, jnp.int32) for a in (pair_home, pair_other, pair_kind, pair_image)]

    readout_row = readout.reshape(1, channels)
    mapped, tiles, kern_t, packed, slope, adjoint, radial_near = pl.pallas_call(
        functools.partial(front_kernel, n_dom, n_rep),
        out_shape=(shape((n_ext, kinds, TILE, channels), BF16), shape((n_ext, 3, TILE), F32),
                   shape((pair_home.shape[0], TILE, TILE), F32), shape((atoms, channels), BF16),
                   shape((atoms, channels), BF16), shape((own, TILE, channels), BF16),
                   shape(radial.shape, BF16)),
        in_specs=[HBM] * 11,
        out_specs=(VMEM,) * 7,
        scratch_shapes=[
            pltpu.VMEM(features.shape, BF16), pltpu.VMEM(positions.shape, F32),
            pltpu.VMEM(send_rows.shape, jnp.int32),
            pltpu.VMEM(mixing.shape, BF16), pltpu.VMEM(readout_row.shape, F32), *pair_tables(),
            pltpu.VMEM((2, TILE, channels), BF16), pltpu.VMEM((2, 3, TILE), F32),
            pltpu.VMEM((4, TILE, channels), BF16), pltpu.VMEM((4, 3, TILE), F32),
            pltpu.VMEM((n_ext, 3, TILE, TILE), F32),
            pltpu.VMEM((pair_home.shape[0], atoms, TILE), BF16), pltpu.VMEM((atoms, channels), F32),
            *[pltpu.VMEM((n_rep, share, channels), BF16)] * 4,
            dma((11,)), *[dma((4,)) for _ in range(8)], *[dma((n_rep,)) for _ in range(6)],
        ],
        compiler_params=params(0),
        name="front",
    )(*[pltpu.with_memory_space_constraint(a, pltpu.HBM) for a in (
        features, positions, send_rows, radial, mixing, readout_row, decay, pair_home, pair_other, pair_kind,
        pair_image)])

    gfeat, side, mix = pl.pallas_call(
        functools.partial(backward_kernel, n_rep),
        out_shape=(shape((n_ext, 2, TILE, channels // 2), BF16), shape((n_ext, 16, TILE), F32),
                   shape((n_dom, channels // n_dom, channels // n_rep), F32)),
        in_specs=[HBM] * 5 + [VMEM] * 7,
        out_specs=(VMEM,) * 3,
        scratch_shapes=[
            *pair_tables(), pltpu.VMEM((n_ext, 80, 2 * TILE), BF16),
            pltpu.VMEM((n_ext, 8, TILE), F32), pltpu.VMEM((n_ext, 8, TILE), F32),
            pltpu.VMEM((n_ext, TILE, channels), F32), dma((5,)),
        ],
        compiler_params=params(),
        name="backward_pairs",
    )(*[pltpu.with_memory_space_constraint(a, pltpu.HBM) for a in (
        decay, pair_home, pair_other, pair_kind, pair_image)],
      tiles, mapped, kern_t, adjoint, radial_near, packed, slope)

    mix_rows, mix_cols = channels // n_dom, channels // n_rep
    results = pl.pallas_call(
        functools.partial(return_kernel, n_dom, n_rep),
        out_shape=(shape((atoms, channels), BF16), shape((3, atoms), F32), shape((6, atoms), F32),
                   shape((mix_rows, mix_cols), F32)),
        in_specs=[VMEM] * 4,
        out_specs=(VMEM,) * 4,
        scratch_shapes=[
            pltpu.VMEM((3, 2, TILE, channels // 2), BF16), pltpu.VMEM((3, 16, TILE), F32),
            pltpu.VMEM((3, 2, TILE, channels // 2), BF16), pltpu.VMEM((3, 16, TILE), F32),
            pltpu.VMEM((3, 2, TILE, channels // 2), BF16), pltpu.VMEM((3, 2, 16, TILE), F32),
            pltpu.VMEM((n_dom, mix_rows, mix_cols), F32), pltpu.VMEM((n_rep, atoms, channels // 2), BF16),
            pltpu.VMEM((16, atoms), F32), pltpu.VMEM((16, atoms), F32),
            *[dma((3,)) for _ in range(4)], *[dma((3, 2)) for _ in range(4)],
            dma((n_dom,)), dma((n_dom,)), dma((n_rep,)), dma((n_rep,)), dma, dma,
        ],
        compiler_params=params(2),
        name="return_gradients",
    )(gfeat, side, mix, send_rows)
    return pl.pallas_call(
        copy_out,
        out_shape=tuple(shape(a.shape, a.dtype) for a in results),
        in_specs=[VMEM] * 4,
        out_specs=(HBM,) * 4,
        scratch_shapes=[dma((4,))],
        compiler_params=pltpu.CompilerParams(vmem_limit_bytes=4 << 20),
        name="copy_out",
    )(*results)


def solution(mesh):
    in_specs = (
        P("dom", None),
        P(None, "dom"),
        P(),
        P(),
        P(),
        P(),
        P(None, "dom"),
        P(("dom", "rep")),
        P(("dom", "rep")),
        P(("dom", "rep")),
        P(None, ("dom", "rep")),
    )
    out_specs = (P("dom", None), P(None, "dom"), P(None, "dom"), P("dom", "rep"))
    body = functools.partial(on_device, mesh.shape["dom"], mesh.shape["rep"])
    return jax.shard_map(body, mesh=mesh, in_specs=in_specs, out_specs=out_specs, check_vma=False)
```

profile of v0, /device:TPU:0, one launch (start us, length us, event | category | flops | bytes accessed | tf_op | source)
XLA Modules:
  0.0 50.1 jit_solution(16162524913796425888)
XLA Ops:
  0.6 25.3 %front.1 = (bf16[6,8,128,256]{3,2,1,0:T(8,128)(2,1)S(1)}, f32[6,3,128]{2,1,0:T(4,128)S(1)}, f32[48,128,128]{2,1,0:T(8,128)S(1)}, bf16[256,256]{1,0:T(8,128)(2,1)...) custom-call(bf16[256,256]{1,0:T(8,128)(2,1)} %feat_h.1, ...), custom_call_target="tpu_custom_call" | custom-call | tf_op jit(solution)/shard_map/front/pallas_call | solution.py:480
  25.9 0.0 copy-start
  25.9 8.9 %backward_pairs.1 = (bf16[6,2,128,128]{3,2,1,0:T(8,128)(2,1)S(1)}, f32[6,16,128]{2,1,0:T(8,128)S(1)}, f32[8,32,64]{2,1,0:T(8,128)S(1)}) custom-call(f32[8]{0:T(128)} %decay_h.3, s32[48]{0:T(128)} %home_h.3, s32[48]{0:T(128)} %other_h.3, s32[48]{0:T(128)} %kind_h.3, s32[3,48]{1,0:T(4,128)} %image_h.3, f32[6,3,128]{2,1,0:T(4,128)S(1)} %get-tuple-element.18.tiles, ...), custom_call_target="tpu_custom_call" | custom-call | tf_op jit(solution)/shard_map/backward_pairs/pallas_call | solution.py:505
  34.9 0.0 copy-done
  34.9 14.5 %return_gradients.1 = (bf16[256,256]{1,0:T(8,128)(2,1)S(1)}, f32[3,256]{1,0:T(4,128)S(1)}, f32[6,256]{1,0:T(8,128)S(1)}, f32[32,64]{1,0:T(8,128)S(1)}) custom-call(bf16[6,2,128,128]{3,2,1,0:T(8,128)(2,1)S(1)} %get-tuple-element.25.gfeat, f32[6,16,128]{2,1,0:T(8,128)S(1)} %get-tuple-element.26.side, f32[8,32,64]{2,1,0:T(8,128)S(1)} %get-tuple-element.27.mix, ...), custom_call_target="tpu_custom_call" | custom-call | tf_op jit(solution)/shard_map/return_gradients/pallas_call | solution.py:523
  49.4 0.7 %copy_out.1 = (bf16[256,256]{1,0:T(8,128)(2,1)}, f32[3,256]{1,0:T(4,128)}, f32[6,256]{1,0:T(8,128)}, f32[32,64]{1,0:T(8,128)}) custom-call(bf16[256,256]{1,0:T(8,128)(2,1)S(1)} %get-tuple-element.28.a, f32[3,256]{1,0:T(4,128)S(1)} %get-tuple-element.29.b, f32[6,256]{1,0:T(8,128)S(1)} %get-tuple-element.30.c, f32[32,64]{1,0:T(8,128)S(1)} %get-tuple-element.31.d), custom_call_target="tpu_custom_call" | custom-call | tf_op jit(solution)/shard_map/copy_out/pallas_call | solution.py:541
Async XLA Ops:
  25.9 8.9 %copy-start = (s32[4,128]{1,0:T(4,128)S(1)}, s32[4,128]{1,0:T(4,128)}, u32[]{:S(2)}) copy-start(s32[4,128]{1,0:T(4,128)} %rows.1) | copy-start | bytes 6148
where the time goes:
time: 50.9 us; the launch traced here: 50.1 us
  Pallas kernels  49.4 us (97%)
  between operations  0.67 us (1%)
    pallas_call x1, Pallas kernels, on_device(): pl.pallas_call(functools.partial(front_kernel, n_dom, n_rep), out_shape=(...  25.3 us
    pallas_call x1, Pallas kernels, on_device(): pl.pallas_call(functools.partial(return_kernel, n_dom, n_rep), out_shape=...  14.5 us
    pallas_call x1, Pallas kernels, on_device(): pl.pallas_call(functools.partial(backward_kernel, n_rep), out_shape=(shap...  8.9 us

commit v1 on v0

v1 whole, which is shorter than its diff:
```python
import functools
import types

import jax
import jax.numpy as jnp
from jax import lax
from jax.experimental import pallas as pl
from jax.experimental.pallas import tpu as pltpu
from jax.sharding import PartitionSpec as P

TILE = 128
OFFSETS = (1, -1, 2, -2)
CELL = 2.0
GROUP = 4
FORWARD_GROUP = 8
BACK_GROUP = 12
F32 = jnp.float32
BF16 = jnp.bfloat16
MESH = pl.DeviceIdType.MESH
VMEM = pl.BlockSpec(memory_space=pltpu.VMEM)
HBM = pl.BlockSpec(memory_space=pltpu.HBM)
INPUTS = ("feat_h", "pos_h", "rows_h", "radial_h", "mixing_h", "readout_h", "decay_h", "home_h", "other_h",
          "kind_h", "image_h", "home_row_h", "other_row_h", "kind_row_h")
OUTPUTS = ("out_feat", "out_force", "out_virial", "out_mix")


def nt(a, b):
    return lax.dot_general(a, b, (((1,), (1,)), ((), ())), preferred_element_type=F32)


def tn(a, b):
    return lax.dot_general(a, b, (((0,), (0,)), ((), ())), preferred_element_type=F32)


def mm(a, b):
    return jnp.dot(a, b, preferred_element_type=F32)


def split3(x):
    hi = x.astype(BF16)
    rest = x - hi.astype(F32)
    mid = rest.astype(BF16)
    low = (rest - mid.astype(F32)).astype(BF16)
    return hi, mid, low


def order_pairs(seg, lanes, subs):
    row = jnp.broadcast_to(seg, (TILE, TILE))
    col = jnp.transpose(row)
    before = (col < row) | ((col == row) & (subs < lanes))
    rank = jnp.sum(before.astype(jnp.int32), axis=0, keepdims=True)
    rank = jnp.transpose(jnp.broadcast_to(rank, (TILE, TILE)))
    order = jnp.sum(jnp.where(rank == lanes, subs, 0), axis=0, keepdims=True)
    upto = jnp.sum((col <= lanes).astype(jnp.int32), axis=0, keepdims=True)
    below = jnp.sum((col < lanes).astype(jnp.int32), axis=0, keepdims=True)
    return order, jnp.where(upto > below, upto, 0)


def kernel(names, n_dom, n_rep, *refs):
    m = types.SimpleNamespace(**dict(zip(names, refs)))
    d = lax.axis_index("dom")
    r = lax.axis_index("rep")
    y = lax.div(r, 2)
    c = lax.rem(r, 2)
    mate = 1 - c
    partner = r + 1 - 2 * c
    across = r + 2 - 4 * y
    atoms, channels = m.feat.shape
    own = atoms // TILE
    pairs = m.home.shape[0]
    kinds = m.radial.shape[0]
    n_ext = m.tiles.shape[0]

    def dom_at(o):
        return lax.rem(d + o + n_dom, n_dom)

    def at(dom, rep):
        return {"dom": dom, "rep": rep}

    loads = [pltpu.make_async_copy(src, dst, m.load.at[i]) for i, (src, dst) in enumerate((
        (m.rows_h, m.rows), (m.feat_h, m.feat), (m.pos_h, m.pos), (m.home_row_h, m.home_row),
        (m.other_row_h, m.other_row), (m.kind_row_h, m.kind_row), (m.radial_h, m.radial), (m.decay_h, m.decay),
        (m.home_h, m.home), (m.other_h, m.other), (m.kind_h, m.kind), (m.image_h, m.image),
        (m.mixing_h, m.mixing), (m.readout_h, m.readout)))]
    for copy in loads:
        copy.start()
    barrier = pltpu.get_barrier_semaphore()
    mine = (c + 1, -(c + 1))
    theirs = (2 - c, c - 2)
    peers = [lax.rem(r + i, n_rep) for i in range(1, n_rep)]

    def hello(dom, rep):
        pl.semaphore_signal(barrier, inc=1, device_id=at(dom, rep), device_id_type=MESH)

    def greet(i, _):
        hello(lax.rem(d + i, n_dom), r)
        return 0

    lax.fori_loop(1, n_dom, greet, 0)
    for o in mine:
        hello(dom_at(o), partner)
        hello(dom_at(o), across)
    for o in theirs:
        hello(dom_at(o), partner)
    for q in peers:
        hello(d, q)

    started = []

    def push(src, dst, ss, rs, target):
        copy = pltpu.make_async_remote_copy(src, dst, ss, rs, device_id=target, device_id_type=MESH)
        copy.start()
        started.append(copy)

    def take(dst, ss, rs):
        pltpu.make_async_remote_copy(dst, dst, ss, rs, device_id=at(d, partner), device_id_type=MESH).wait_recv()

    for copy in loads[:3]:
        copy.wait()
    iota = lax.broadcasted_iota(jnp.int32, (atoms, TILE), 0)
    hots = []
    for q in range(2):
        hot = (iota == m.rows[pl.ds(2 * c + q, 1), :]).astype(F32)
        hots.append(hot.astype(BF16))
        m.sendp[q] = jnp.dot(m.pos[...], hot, precision=lax.Precision.HIGHEST, preferred_element_type=F32)
    pl.semaphore_wait(barrier, 6 + n_rep - 1 + n_dom - 1)
    for q in range(2):
        for i, rep in enumerate((r, partner)):
            push(m.sendp.at[q], m.recvp.at[2 * c + q], m.s_pos.at[q, i], m.r_pos.at[2 * c + q],
                 at(dom_at(mine[q]), rep))
    for q in range(2):
        m.sendf[q] = tn(hots[q], m.feat[...]).astype(BF16)
        push(m.sendf.at[q], m.ext.at[own + 2 * c + q], m.s_feat.at[q], m.r_feat.at[2 * c + q],
             at(dom_at(mine[q]), r))

    for copy in loads[3:6]:
        copy.wait()
    m.raw[...] = jnp.zeros_like(m.raw)
    for i, src in enumerate((m.home_row, m.kind_row, m.other_row)):
        m.raw[i:i + 1, :pairs] = src[...]
    raw = m.raw[...]
    lanes = lax.broadcasted_iota(jnp.int32, (TILE, TILE), 1)
    subs = lax.broadcasted_iota(jnp.int32, (TILE, TILE), 0)
    real = lanes[0:1] < pairs
    order_f, end_f = order_pairs(jnp.where(real, raw[0:1] * kinds + raw[1:2], TILE), lanes, subs)
    order_b, end_b = order_pairs(jnp.where(real, raw[2:3], TILE), lanes, subs)
    m.plan_v[...] = jnp.concatenate(
        [order_f, order_b, end_f, end_b, jnp.zeros((4, TILE), jnp.int32)], axis=0)
    plan_copy = pltpu.make_async_copy(m.plan_v, m.plan, m.s_plan)
    plan_copy.start()

    def columns(j):
        for x in range(3):
            m.col[j, x] = jnp.transpose(jnp.broadcast_to(m.tiles[j][x:x + 1, :], (TILE, TILE)))

    def table(j):
        pos = m.tiles[j]
        x, yy, z = pos[0:1, :], pos[1:2, :], pos[2:3, :]
        zero = jnp.zeros((2, TILE), F32)
        one_rows = jnp.concatenate([x, yy, z, x, x, yy, zero], axis=0)
        two_rows = jnp.concatenate([x, yy, z, yy, z, z, zero], axis=0)
        m.first[j] = one_rows
        m.second[j] = two_rows
        stack = jnp.concatenate([one_rows * two_rows, one_rows, two_rows], axis=0)
        parts = [v.astype(F32) for v in split3(stack)]
        m.moments[j] = jnp.concatenate(
            [parts[0], jnp.ones((8, TILE), F32), parts[1], parts[2]], axis=0).astype(BF16)

    for j in range(own):
        m.tiles[j] = m.pos[:, j * TILE:(j + 1) * TILE]
        m.ext[j] = m.feat[j * TILE:(j + 1) * TILE, :]
        columns(j)
        table(j)
    m.sums[0] = jnp.zeros_like(m.sums[0])
    m.far[0] = jnp.zeros_like(m.far[0])
    m.near[...] = jnp.zeros_like(m.near)
    for copy in loads[6:]:
        copy.wait()
    for t in range(4):
        take(m.recvp.at[t], m.s_pos.at[0, 0], m.r_pos.at[t])
        m.tiles[own + t] = m.recvp[t]
        columns(own + t)
        table(own + t)

    def kernels(g, _):
        for u in range(GROUP):
            p = g * GROUP + u
            h, o, k = m.home[p], m.other[p], m.kind[p]
            shift = [m.image[x, p].astype(F32) * CELL for x in range(3)]
            rate = -m.decay[k]
            row, back = m.tiles[o], m.tiles[h]
            d2 = None
            e2 = None
            for x in range(3):
                sep = (row[x:x + 1, :] + shift[x]) - m.col[h, x]
                d2 = sep * sep if d2 is None else d2 + sep * sep
                sep = m.col[o, x] - (back[x:x + 1, :] - shift[x])
                e2 = sep * sep if e2 is None else e2 + sep * sep
            m.kern_ab[p] = jnp.exp(d2 * rate).astype(BF16)
            m.kern_ba[p] = jnp.exp(e2 * rate)
        return 0

    half_steps = pairs // GROUP // 2
    lax.fori_loop(0, half_steps, kernels, 0)
    for q in range(2):
        t = 2 * c + q
        take(m.ext.at[own + t], m.s_feat.at[q], m.r_feat.at[t])
        push(m.ext.at[own + t], m.ext.at[own + t], m.s_relay.at[q], m.r_relay.at[t], at(d, partner))
    lax.fori_loop(half_steps, pairs // GROUP, kernels, 0)
    plan_copy.wait()
    for q in range(2):
        t = 2 * mate + q
        take(m.ext.at[own + t], m.s_relay.at[q], m.r_relay.at[t])

    def pair_at(row, i):
        return jnp.clip(m.plan[row, i], 0, pairs - 1)

    def sum_at(row, i):
        return jnp.clip(m.plan[row, i], 0, pairs)

    def seg_f(p):
        return m.home[p] * kinds + m.kind[p]

    def forward(g, _):
        acc = m.sums[g * FORWARD_GROUP]
        for u in range(FORWARD_GROUP):
            i = g * FORWARD_GROUP + u
            p = pair_at(0, i)
            last = pair_at(0, jnp.maximum(i - 1, 0))
            keep = (seg_f(p) == seg_f(last)).astype(F32)
            acc = acc * keep + mm(m.kern_ab[p], m.ext[m.other[p]])
            m.sums[i + 1] = acc
        return 0

    lax.fori_loop(0, pairs // FORWARD_GROUP, forward, 0)

    def message(h):
        left = [m.sums[sum_at(2, h * kinds + k)].astype(BF16) for k in range(kinds)]
        return mm(jnp.concatenate(left, axis=1), m.radial[...].reshape(kinds * channels, channels))

    m.msg[...] = message(mate).astype(BF16)
    push(m.msg, m.msg_in, m.s_msg.at[0], m.r_msg.at[0], at(d, partner))
    value = message(c)
    take(m.msg_in, m.s_msg.at[0], m.r_msg.at[0])
    value = (value + m.msg_in[...].astype(F32)).astype(BF16)
    m.chip[...] = value
    push(m.chip, m.chip_in, m.s_msg.at[1], m.r_msg.at[1], at(d, across))
    take(m.chip_in, m.s_msg.at[1], m.r_msg.at[1])
    low = (value.astype(F32) + m.chip_in[...].astype(F32)).astype(BF16)
    mixed = mm(low, m.mixing[...])
    sig = jax.nn.sigmoid(mixed)
    slope = (m.readout[...] * sig * (1.0 + mixed * (1.0 - sig))).astype(BF16)
    adj = nt(slope, m.mixing[...]).astype(BF16)
    m.adjoint[c] = adj
    push(m.adjoint.at[c], m.adjoint.at[c], m.s_adj.at[0], m.r_adj.at[0], at(d, partner))
    m.slope[c] = slope
    push(m.slope.at[c], m.slope.at[c], m.s_adj.at[1], m.r_adj.at[1], at(d, partner))
    m.packed[c] = low
    push(m.packed.at[c], m.packed.at[c], m.s_adj.at[2], m.r_adj.at[2], at(d, partner))

    def spread(h):
        value = m.adjoint[h]
        for k in range(kinds):
            m.weights[h * kinds + k] = nt(value, m.radial[k]).astype(BF16)

    spread(c)
    take(m.adjoint.at[mate], m.s_adj.at[0], m.r_adj.at[0])
    spread(mate)

    sub = lax.broadcasted_iota(jnp.int32, (8, TILE), 0)
    is_x1, is_y1 = (sub == 0) | (sub == 3) | (sub == 4), (sub == 1) | (sub == 5)
    is_x2, is_y2 = (sub == 0), (sub == 1) | (sub == 3)

    def combine(res, a, b):
        quad = res[0:8] + res[32:40] + res[56:64]
        lin1 = res[8:16] + res[40:48] + res[64:72]
        lin2 = res[16:24] + res[48:56] + res[72:80]
        one = res[24:32]
        force = lin1 - a * one
        virial = -0.5 * (quad - a * lin2 - b * lin1 + a * b * one)
        return jnp.concatenate([force, virial], axis=0)

    def backward(g, _):
        found = []
        for u in range(BACK_GROUP):
            i = g * BACK_GROUP + u
            p = pair_at(1, i)
            last = pair_at(1, jnp.maximum(i - 1, 0))
            h, o, k = m.home[p], m.other[p], m.kind[p]
            keep = (o == m.other[last]).astype(F32)
            kern = m.kern_ba[p]
            right = m.weights[h * kinds + k]
            weight = ((-2.0 * m.decay[k]) * kern * nt(m.ext[o], right)).astype(BF16)
            found.append((i, p, h, o, keep, kern.astype(BF16), right, weight))
        acc = m.sums[g * BACK_GROUP]
        far = m.far[g * BACK_GROUP]
        near = [m.near[j] for j in range(own)]
        for i, p, h, o, keep, kern, right, weight in found:
            shift = [m.image[x, p].astype(F32) * CELL for x in range(3)]
            s1 = jnp.where(is_x1, shift[0], jnp.where(is_y1, shift[1], shift[2]))
            s2 = jnp.where(is_x2, shift[0], jnp.where(is_y2, shift[1], shift[2]))
            near_side = combine(mm(m.moments[o], weight), m.first[h] - s1, m.second[h] - s2)
            far_side = combine(nt(m.moments[h], weight), m.first[o] + s1, m.second[o] + s2)
            for j in range(own):
                near[j] = near[j] + near_side * (h == j).astype(F32)
            far = far * keep + far_side
            m.far[i + 1] = far
            acc = acc * keep + mm(kern, right)
            m.sums[i + 1] = acc
        for j in range(own):
            m.near[j] = near[j]
        return 0

    lax.fori_loop(0, pairs // BACK_GROUP, backward, 0)

    def settle(j, local):
        at_end = sum_at(3, j)
        total = m.sums[at_end]
        for half in range(2):
            m.gfeat[j, half] = total[:, half * TILE:(half + 1) * TILE].astype(BF16)
        m.side[j] = m.far[at_end] + m.near[j] if local else m.far[at_end]

    for slot, j in ((1, 2 + 2 * mate), (2, 3 + 2 * mate), (0, mate)):
        settle(j, slot == 0)
        push(m.gfeat.at[j], m.gp.at[slot], m.s_gp.at[slot], m.r_gp.at[slot], at(d, partner))
        push(m.side.at[j], m.gs.at[slot], m.s_gs.at[slot], m.r_gs.at[slot], at(d, partner))
    for slot, j in ((1, 2 + 2 * c), (2, 3 + 2 * c), (0, c)):
        settle(j, slot == 0)
    take(m.slope.at[mate], m.s_adj.at[1], m.r_adj.at[1])
    take(m.packed.at[mate], m.s_adj.at[2], m.r_adj.at[2])
    share = channels // n_rep
    pick = (lax.broadcasted_iota(jnp.int32, (channels, share), 0)
            == lax.broadcasted_iota(jnp.int32, (channels, share), 1) + r * share).astype(BF16)
    cols = mm(m.slope[...].reshape(atoms, channels), pick).astype(BF16)
    m.mix[...] = tn(m.packed[...].reshape(atoms, channels), cols).reshape(m.mix.shape)
    for slot, j in ((1, 2 + 2 * c), (2, 3 + 2 * c), (0, c)):
        take(m.gp.at[slot], m.s_gp.at[slot], m.r_gp.at[slot])
        take(m.gs.at[slot], m.s_gs.at[slot], m.r_gs.at[slot])
        m.sb[slot] = (m.gfeat[j].astype(F32) + m.gp[slot].astype(F32)).astype(BF16)
        m.ss[slot] = m.side[j] + m.gs[slot]
        for half in ((0, 1) if slot else (1 - y,)):
            dest = at(dom_at(-mine[slot - 1]) if slot else d, 2 * half + c)
            push(m.sb.at[slot, half], m.rf.at[slot, y], m.s_rf.at[slot, half], m.r_rf.at[slot, y], dest)
            push(m.ss.at[slot], m.rs.at[slot, y], m.s_rs.at[slot, half], m.r_rs.at[slot, y], dest)

    def mix_copy(i):
        to = lax.rem(d + i, n_dom)
        return pltpu.make_async_remote_copy(m.mix.at[to], m.rm.at[d], m.s_mix.at[i], m.r_mix.at[d],
                                            device_id=at(to, r), device_id_type=MESH)

    lax.fori_loop(1, n_dom, lambda i, _: (mix_copy(i).start(), 0)[1], 0)
    take(m.rf.at[0, 1 - y], m.s_rf.at[0, 0], m.r_rf.at[0, 1 - y])
    take(m.rs.at[0, 1 - y], m.s_rs.at[0, 0], m.r_rs.at[0, 1 - y])
    feat_self = m.sb[0, y].astype(F32) + m.rf[0, 1 - y].astype(F32)
    side_self = m.ss[0] + m.rs[0, 1 - y]
    is_low = c == 0
    zero = jnp.zeros_like(feat_self)
    total = jnp.concatenate([jnp.where(is_low, feat_self, zero), jnp.where(is_low, zero, feat_self)], axis=0)
    zside = jnp.zeros_like(side_self)
    total_side = jnp.concatenate([jnp.where(is_low, side_self, zside), jnp.where(is_low, zside, side_self)],
                                 axis=1)
    for q in range(2):
        hot = (iota == m.rows[pl.ds(2 * c + q, 1), :]).astype(F32).astype(BF16)
        slot = 1 + q
        got = None
        for s in range(2):
            take(m.rf.at[slot, s], m.s_rf.at[0, 0], m.r_rf.at[slot, s])
            take(m.rs.at[slot, s], m.s_rs.at[0, 0], m.r_rs.at[slot, s])
            total = total + mm(hot, m.rf[slot, s])
            got = m.rs[slot, s] if got is None else got + m.rs[slot, s]
        for v in split3(got):
            total_side = total_side + nt(v, hot)
    m.part[r] = total.astype(BF16)
    m.pside[...] = total_side
    for i, q in enumerate(peers):
        push(m.part.at[r], m.part.at[r], m.s_part.at[i], m.r_part.at[r], at(d, q))
    push(m.pside, m.qside, m.s_side, m.r_side, at(d, partner))

    def mix_add(i, value):
        frm = lax.rem(d + i, n_dom)
        take(m.rm.at[frm], m.s_mix.at[0], m.r_mix.at[frm])
        return value + m.rm[frm]

    m.out_mix[...] = lax.fori_loop(1, n_dom, mix_add, m.mix[d])
    take(m.qside, m.s_side, m.r_side)
    final = total_side + m.qside[...]
    m.out_force[...] = final[0:3]
    m.out_virial[...] = final[8:14]
    for q in peers:
        take(m.part.at[q], m.s_part.at[0], m.r_part.at[q])
    for half in range(2):
        m.out_feat[:, half * TILE:(half + 1) * TILE] = (
            m.part[2 * half].astype(F32) + m.part[2 * half + 1].astype(F32)).astype(BF16)
    for copy in started:
        copy.wait_send()
    lax.fori_loop(1, n_dom, lambda i, _: (mix_copy(i).wait_send(), 0)[1], 0)


def copy_out(a, b, c, d, a_h, b_h, c_h, d_h, sem):
    copies = [pltpu.make_async_copy(src, dst, sem.at[i])
              for i, (src, dst) in enumerate(((a, a_h), (b, b_h), (c, c_h), (d, d_h)))]
    for copy in copies:
        copy.start()
    for copy in copies:
        copy.wait()


def on_device(n_dom, n_rep, features, positions, radial, mixing, readout, decay, send_rows, pair_home,
              pair_other, pair_kind, pair_image):
    atoms, channels = features.shape
    own = atoms // TILE
    n_ext = own + len(OFFSETS)
    kinds = radial.shape[0]
    pairs = pair_home.shape[0]
    dma = pltpu.SemaphoreType.DMA
    mix_rows, mix_cols = channels // n_dom, channels // n_rep
    half = (2, TILE, channels // 2)
    readout_row = readout.reshape(1, channels)
    pair_rows = [a.reshape(1, pairs) for a in (pair_home, pair_other, pair_kind)]

    scratch = {
        "feat": pltpu.VMEM(features.shape, BF16), "pos": pltpu.VMEM(positions.shape, F32),
        "rows": pltpu.VMEM(send_rows.shape, jnp.int32), "radial": pltpu.VMEM(radial.shape, BF16),
        "mixing": pltpu.VMEM(mixing.shape, BF16), "readout": pltpu.VMEM(readout_row.shape, F32),
        "decay": pltpu.SMEM(decay.shape, F32), "home": pltpu.SMEM(pair_home.shape, jnp.int32),
        "other": pltpu.SMEM(pair_other.shape, jnp.int32), "kind": pltpu.SMEM(pair_kind.shape, jnp.int32),
        "image": pltpu.SMEM(pair_image.shape, jnp.int32),
        "home_row": pltpu.VMEM((1, pairs), jnp.int32), "other_row": pltpu.VMEM((1, pairs), jnp.int32),
        "kind_row": pltpu.VMEM((1, pairs), jnp.int32),
        "raw": pltpu.VMEM((8, TILE), jnp.int32), "plan_v": pltpu.VMEM((8, TILE), jnp.int32),
        "plan": pltpu.SMEM((8, TILE), jnp.int32),
        "sendf": pltpu.VMEM((2, TILE, channels), BF16), "sendp": pltpu.VMEM((2, 3, TILE), F32),
        "recvp": pltpu.VMEM((4, 3, TILE), F32), "ext": pltpu.VMEM((n_ext, TILE, channels), BF16),
        "tiles": pltpu.VMEM((n_ext, 3, TILE), F32), "col": pltpu.VMEM((n_ext, 3, TILE, TILE), F32),
        "moments": pltpu.VMEM((n_ext, 80, TILE), BF16),
        "first": pltpu.VMEM((n_ext, 8, TILE), F32), "second": pltpu.VMEM((n_ext, 8, TILE), F32),
        "kern_ab": pltpu.VMEM((pairs, TILE, TILE), BF16), "kern_ba": pltpu.VMEM((pairs, TILE, TILE), F32),
        "sums": pltpu.VMEM((pairs + 1, TILE, channels), F32), "far": pltpu.VMEM((pairs + 1, 16, TILE), F32),
        "near": pltpu.VMEM((own, 16, TILE), F32),
        "msg": pltpu.VMEM((TILE, channels), BF16), "msg_in": pltpu.VMEM((TILE, channels), BF16),
        "chip": pltpu.VMEM((TILE, channels), BF16), "chip_in": pltpu.VMEM((TILE, channels), BF16),
        "adjoint": pltpu.VMEM((own, TILE, channels), BF16), "slope": pltpu.VMEM((own, TILE, channels), BF16),
        "packed": pltpu.VMEM((own, TILE, channels), BF16),
        "weights": pltpu.VMEM((own * kinds, TILE, channels), BF16),
        "gfeat": pltpu.VMEM((n_ext, *half), BF16), "side": pltpu.VMEM((n_ext, 16, TILE), F32),
        "gp": pltpu.VMEM((3, *half), BF16), "gs": pltpu.VMEM((3, 16, TILE), F32),
        "sb": pltpu.VMEM((3, *half), BF16), "ss": pltpu.VMEM((3, 16, TILE), F32),
        "rf": pltpu.VMEM((3, *half), BF16), "rs": pltpu.VMEM((3, 2, 16, TILE), F32),
        "mix": pltpu.VMEM((n_dom, mix_rows, mix_cols), F32), "rm": pltpu.VMEM((n_dom, mix_rows, mix_cols), F32),
        "part": pltpu.VMEM((n_rep, atoms, channels // 2), BF16),
        "pside": pltpu.VMEM((16, atoms), F32), "qside": pltpu.VMEM((16, atoms), F32),
        "load": dma((len(INPUTS),)), "s_plan": dma, "s_pos": dma((2, 2)), "r_pos": dma((4,)),
        "s_feat": dma((2,)), "r_feat": dma((4,)), "s_relay": dma((2,)), "r_relay": dma((4,)),
        "s_msg": dma((2,)), "r_msg": dma((2,)), "s_adj": dma((3,)), "r_adj": dma((3,)),
        "s_gp": dma((3,)), "r_gp": dma((3,)), "s_gs": dma((3,)), "r_gs": dma((3,)),
        "s_rf": dma((3, 2)), "r_rf": dma((3, 2)), "s_rs": dma((3, 2)), "r_rs": dma((3, 2)),
        "s_mix": dma((n_dom,)), "r_mix": dma((n_dom,)), "s_part": dma((n_rep,)), "r_part": dma((n_rep,)),
        "s_side": dma, "r_side": dma,
    }

    def shape(dims, dtype):
        return jax.ShapeDtypeStruct(dims, dtype)

    results = pl.pallas_call(
        functools.partial(kernel, INPUTS + OUTPUTS + tuple(scratch), n_dom, n_rep),
        out_shape=(shape((atoms, channels), BF16), shape((3, atoms), F32), shape((6, atoms), F32),
                   shape((mix_rows, mix_cols), F32)),
        in_specs=[HBM] * len(INPUTS),
        out_specs=(VMEM,) * 4,
        scratch_shapes=list(scratch.values()),
        compiler_params=pltpu.CompilerParams(collective_id=0, has_side_effects=True, vmem_limit_bytes=48 << 20),
        name="layer",
    )(*[pltpu.with_memory_space_constraint(a, pltpu.HBM) for a in (
        features, positions, send_rows, radial, mixing, readout_row, decay, pair_home, pair_other, pair_kind,
        pair_image, *pair_rows)])
    return pl.pallas_call(
        copy_out,
        out_shape=tuple(shape(a.shape, a.dtype) for a in results),
        in_specs=[VMEM] * 4,
        out_specs=(HBM,) * 4,
        scratch_shapes=[dma((4,))],
        compiler_params=pltpu.CompilerParams(vmem_limit_bytes=4 << 20),
        name="copy_out",
    )(*results)


def solution(mesh):
    in_specs = (
        P("dom", None),
        P(None, "dom"),
        P(),
        P(),
        P(),
        P(),
        P(None, "dom"),
        P(("dom", "rep")),
        P(("dom", "rep")),
        P(("dom", "rep")),
        P(None, ("dom", "rep")),
    )
    out_specs = (P("dom", None), P(None, "dom"), P(None, "dom"), P("dom", "rep"))
    body = functools.partial(on_device, mesh.shape["dom"], mesh.shape["rep"])
    return jax.shard_map(body, mesh=mesh, in_specs=in_specs, out_specs=out_specs, check_vma=False)
```

time: 50.9 us -> 39.5 us (0.78); the launches traced: 50.1 us -> 39.3 us
  Pallas kernels: 49.4 us -> 38.6 us
    pallas_call x3 -> x1, Pallas kernels: 48.7 us -> 37.9 us  [on_device(): pl.pallas_call(functools.partial(kernel, INPUTS + OUTPUTS + tuple(scratch...]
where the time goes in v1:
time: 39.5 us; the launch traced here: 39.3 us
  Pallas kernels  38.6 us (98%)
  between operations  0.64 us (2%)
    pallas_call x1, Pallas kernels, on_device(): pl.pallas_call(functools.partial(kernel, INPUTS + OUTPUTS + tuple(scratch...  37.9 us

profile of v1, /device:TPU:0, one launch (start us, length us, event | category | flops | bytes accessed | tf_op | source)
XLA Modules:
  0.0 39.3 jit_solution(14800604408912298792)
XLA Ops:
  0.6 37.9 %layer.1 = (bf16[256,256]{1,0:T(8,128)(2,1)S(1)}, f32[3,256]{1,0:T(4,128)S(1)}, f32[6,256]{1,0:T(8,128)S(1)}, f32[32,64]{1,0:T(8,128)S(1)}) custom-call(bf16[256,256]{1,0:T(8,128)(2,1)} %refs_0_.1, f32[3,256]{1,0:T(4,128)} %refs_1_.1, s32[4,128]{1,0:T(4,128)} %refs_2_.1, bf16[8,256,256]{2,1,0:T(8,128)(2,1)} %refs_3_.1, bf16[256,256]{1,0:T(8,128)(2,1)} %refs_4_.1, ...), custom_call_target="tpu_custom_call" | custom-call | tf_op jit(solution)/shard_map/layer/pallas_call | solution.py:464
  38.6 0.7 %copy_out.1 = (bf16[256,256]{1,0:T(8,128)(2,1)}, f32[3,256]{1,0:T(4,128)}, f32[6,256]{1,0:T(8,128)}, f32[32,64]{1,0:T(8,128)}) custom-call(bf16[256,256]{1,0:T(8,128)(2,1)S(1)} %get-tuple-element.8.a, f32[3,256]{1,0:T(4,128)S(1)} %get-tuple-element.9.b, f32[6,256]{1,0:T(8,128)S(1)} %get-tuple-element.10.c, f32[32,64]{1,0:T(8,128)S(1)} %get-tuple-element.11.d), custom_call_target="tpu_custom_call" | custom-call | tf_op jit(solution)/shard_map/copy_out/pallas_call | solution.py:476

commit v2 on v1

--- a/solution.py
+++ b/solution.py
@@ -14,6 +14,7 @@
 GROUP = 4
 FORWARD_GROUP = 8
 BACK_GROUP = 12
+SPREAD_GROUP = 8
 F32 = jnp.float32
 BF16 = jnp.bfloat16
 MESH = pl.DeviceIdType.MESH
@@ -82,7 +83,7 @@
         (m.other_row_h, m.other_row), (m.kind_row_h, m.kind_row), (m.radial_h, m.radial), (m.decay_h, m.decay),
         (m.home_h, m.home), (m.other_h, m.other), (m.kind_h, m.kind), (m.image_h, m.image),
         (m.mixing_h, m.mixing), (m.readout_h, m.readout)))]
-    for copy in loads:
+    for copy in loads[:3]:
         copy.start()
     barrier = pltpu.get_barrier_semaphore()
     mine = (c + 1, -(c + 1))
@@ -104,6 +105,8 @@
         hello(dom_at(o), partner)
     for q in peers:
         hello(d, q)
+    for copy in loads[3:]:
+        copy.start()
 
     started = []
 
@@ -123,16 +126,8 @@
         hot = (iota == m.rows[pl.ds(2 * c + q, 1), :]).astype(F32)
         hots.append(hot.astype(BF16))
         m.sendp[q] = jnp.dot(m.pos[...], hot, precision=lax.Precision.HIGHEST, preferred_element_type=F32)
-    pl.semaphore_wait(barrier, 6 + n_rep - 1 + n_dom - 1)
-    for q in range(2):
-        for i, rep in enumerate((r, partner)):
-            push(m.sendp.at[q], m.recvp.at[2 * c + q], m.s_pos.at[q, i], m.r_pos.at[2 * c + q],
-                 at(dom_at(mine[q]), rep))
     for q in range(2):
         m.sendf[q] = tn(hots[q], m.feat[...]).astype(BF16)
-        push(m.sendf.at[q], m.ext.at[own + 2 * c + q], m.s_feat.at[q], m.r_feat.at[2 * c + q],
-             at(dom_at(mine[q]), r))
-
     for copy in loads[3:6]:
         copy.wait()
     m.raw[...] = jnp.zeros_like(m.raw)
@@ -170,34 +165,50 @@
         m.tiles[j] = m.pos[:, j * TILE:(j + 1) * TILE]
         m.ext[j] = m.feat[j * TILE:(j + 1) * TILE, :]
         columns(j)
-        table(j)
+    pl.semaphore_wait(barrier, 6 + n_rep - 1 + n_dom - 1)
+    for q in range(2):
+        for i, rep in enumerate((r, partner)):
+            push(m.sendp.at[q], m.recvp.at[2 * c + q], m.s_pos.at[q, i], m.r_pos.at[2 * c + q],
+                 at(dom_at(mine[q]), rep))
+    for q in range(2):
+        push(m.sendf.at[q], m.ext.at[own + 2 * c + q], m.s_feat.at[q], m.r_feat.at[2 * c + q],
+             at(dom_at(mine[q]), r))
+
     m.sums[0] = jnp.zeros_like(m.sums[0])
     m.far[0] = jnp.zeros_like(m.far[0])
     m.near[...] = jnp.zeros_like(m.near)
+    m.eye[...] = (lax.broadcasted_iota(jnp.int32, m.eye.shape, 0)
+                  == lax.broadcasted_iota(jnp.int32, m.eye.shape, 1)).astype(F32).astype(BF16)
+    for j in range(own):
+        table(j)
     for copy in loads[6:]:
         copy.wait()
     for t in range(4):
         take(m.recvp.at[t], m.s_pos.at[0, 0], m.r_pos.at[t])
         m.tiles[own + t] = m.recvp[t]
-        columns(own + t)
-        table(own + t)
 
     def kernels(g, _):
         for u in range(GROUP):
             p = g * GROUP + u
             h, o, k = m.home[p], m.other[p], m.kind[p]
-            shift = [m.image[x, p].astype(F32) * CELL for x in range(3)]
-            rate = -m.decay[k]
-            row, back = m.tiles[o], m.tiles[h]
+            row = m.tiles[o]
             d2 = None
-            e2 = None
             for x in range(3):
-                sep = (row[x:x + 1, :] + shift[x]) - m.col[h, x]
+                sep = (row[x:x + 1, :] + m.image[x, p].astype(F32) * CELL) - m.col[h, x]
                 d2 = sep * sep if d2 is None else d2 + sep * sep
-                sep = m.col[o, x] - (back[x:x + 1, :] - shift[x])
-                e2 = sep * sep if e2 is None else e2 + sep * sep
-            m.kern_ab[p] = jnp.exp(d2 * rate).astype(BF16)
-            m.kern_ba[p] = jnp.exp(e2 * rate)
+            m.kern_ab[p] = jnp.exp(d2 * (-m.decay[k])).astype(BF16)
+        return 0
+
+    def transposed(g, _):
+        for u in range(GROUP):
+            p = g * GROUP + u
+            h, o, k = m.home[p], m.other[p], m.kind[p]
+            row = m.tiles[h]
+            d2 = None
+            for x in range(3):
+                sep = m.col[o, x] - (row[x:x + 1, :] - m.image[x, p].astype(F32) * CELL)
+                d2 = sep * sep if d2 is None else d2 + sep * sep
+            m.kern_ba[p] = jnp.exp(d2 * (-m.decay[k]))
         return 0
 
     half_steps = pairs // GROUP // 2
@@ -241,10 +252,14 @@
     m.msg[...] = message(mate).astype(BF16)
     push(m.msg, m.msg_in, m.s_msg.at[0], m.r_msg.at[0], at(d, partner))
     value = message(c)
+    for t in range(4):
+        columns(own + t)
+        table(own + t)
     take(m.msg_in, m.s_msg.at[0], m.r_msg.at[0])
     value = (value + m.msg_in[...].astype(F32)).astype(BF16)
     m.chip[...] = value
     push(m.chip, m.chip_in, m.s_msg.at[1], m.r_msg.at[1], at(d, across))
+    lax.fori_loop(0, pairs // GROUP, transposed, 0)
     take(m.chip_in, m.s_msg.at[1], m.r_msg.at[1])
     low = (value.astype(F32) + m.chip_in[...].astype(F32)).astype(BF16)
     mixed = mm(low, m.mixing[...])
@@ -280,22 +295,31 @@
         virial = -0.5 * (quad - a * lin2 - b * lin1 + a * b * one)
         return jnp.concatenate([force, virial], axis=0)
 
+    def pair_b(i):
+        p = pair_at(1, i)
+        last = pair_at(1, jnp.maximum(i - 1, 0))
+        keep = (m.other[p] == m.other[last]).astype(F32)
+        return p, m.home[p], m.other[p], m.kind[p], keep
+
+    def spread_back(g, _):
+        acc = m.sums[g * SPREAD_GROUP]
+        for u in range(SPREAD_GROUP):
+            i = g * SPREAD_GROUP + u
+            p, h, _, k, keep = pair_b(i)
+            acc = acc * keep + mm(m.kern_ba[p].astype(BF16), m.weights[h * kinds + k])
+            m.sums[i + 1] = acc
+        return 0
+
     def backward(g, _):
         found = []
         for u in range(BACK_GROUP):
             i = g * BACK_GROUP + u
-            p = pair_at(1, i)
-            last = pair_at(1, jnp.maximum(i - 1, 0))
-            h, o, k = m.home[p], m.other[p], m.kind[p]
-            keep = (o == m.other[last]).astype(F32)
-            kern = m.kern_ba[p]
-            right = m.weights[h * kinds + k]
-            weight = ((-2.0 * m.decay[k]) * kern * nt(m.ext[o], right)).astype(BF16)
-            found.append((i, p, h, o, keep, kern.astype(BF16), right, weight))
-        acc = m.sums[g * BACK_GROUP]
+            p, h, o, k, keep = pair_b(i)
+            grad = nt(m.ext[o], m.weights[h * kinds + k])
+            found.append((i, p, h, o, keep, ((-2.0 * m.decay[k]) * m.kern_ba[p] * grad).astype(BF16)))
         far = m.far[g * BACK_GROUP]
         near = [m.near[j] for j in range(own)]
-        for i, p, h, o, keep, kern, right, weight in found:
+        for i, p, h, o, keep, weight in found:
             shift = [m.image[x, p].astype(F32) * CELL for x in range(3)]
             s1 = jnp.where(is_x1, shift[0], jnp.where(is_y1, shift[1], shift[2]))
             s2 = jnp.where(is_x2, shift[0], jnp.where(is_y2, shift[1], shift[2]))
@@ -305,42 +329,59 @@
                 near[j] = near[j] + near_side * (h == j).astype(F32)
             far = far * keep + far_side
             m.far[i + 1] = far
-            acc = acc * keep + mm(kern, right)
-            m.sums[i + 1] = acc
         for j in range(own):
             m.near[j] = near[j]
         return 0
 
-    lax.fori_loop(0, pairs // BACK_GROUP, backward, 0)
-
-    def settle(j, local):
-        at_end = sum_at(3, j)
-        total = m.sums[at_end]
-        for half in range(2):
-            m.gfeat[j, half] = total[:, half * TILE:(half + 1) * TILE].astype(BF16)
-        m.side[j] = m.far[at_end] + m.near[j] if local else m.far[at_end]
-
-    for slot, j in ((1, 2 + 2 * mate), (2, 3 + 2 * mate), (0, mate)):
-        settle(j, slot == 0)
+    lax.fori_loop(0, pairs // SPREAD_GROUP, spread_back, 0)
+
+    share = channels // n_rep
+    away = ((1, 2 + 2 * mate), (2, 3 + 2 * mate), (0, mate))
+    held = ((1, 2 + 2 * c), (2, 3 + 2 * c), (0, c))
+
+    def settle(slots):
+        total = jnp.concatenate([m.sums[sum_at(3, j)].astype(BF16) for _, j in slots], axis=0)
+        turned = nt(m.eye[:channels, :channels], total).astype(BF16)
+        for i, (_, j) in enumerate(slots):
+            m.gfeat[j] = turned[:, i * TILE:(i + 1) * TILE].reshape(n_rep, share, TILE)
+
+    settle(away)
+    for slot, j in away:
         push(m.gfeat.at[j], m.gp.at[slot], m.s_gp.at[slot], m.r_gp.at[slot], at(d, partner))
+    settle(held)
+    half_back = pairs // BACK_GROUP // 2
+    lax.fori_loop(0, half_back, backward, 0)
+    for slot, j in held:
+        take(m.gp.at[slot], m.s_gp.at[slot], m.r_gp.at[slot])
+        m.sb[slot] = (m.gfeat[j].astype(F32) + m.gp[slot].astype(F32)).astype(BF16)
+        if slot:
+            t = 2 * c + slot - 1
+            for q in range(n_rep):
+                push(m.sb.at[slot, q], m.rf.at[t, y], m.s_rf.at[slot - 1, q], m.r_rf.at[t, y],
+                     at(dom_at(-mine[slot - 1]), q))
+    for i, q in enumerate(peers):
+        push(m.sb.at[0, q], m.ro.at[c, y], m.s_ro.at[i], m.r_ro.at[c, y], at(d, q))
+    m.ro[c, y] = m.sb[0, r]
+    lax.fori_loop(half_back, pairs // BACK_GROUP, backward, 0)
+    def settle_side(slot, j):
+        m.side[j] = m.far[sum_at(3, j)] if slot else m.far[sum_at(3, j)] + m.near[j]
+
+    for slot, j in away:
+        settle_side(slot, j)
         push(m.side.at[j], m.gs.at[slot], m.s_gs.at[slot], m.r_gs.at[slot], at(d, partner))
-    for slot, j in ((1, 2 + 2 * c), (2, 3 + 2 * c), (0, c)):
-        settle(j, slot == 0)
+    for slot, j in held:
+        settle_side(slot, j)
     take(m.slope.at[mate], m.s_adj.at[1], m.r_adj.at[1])
     take(m.packed.at[mate], m.s_adj.at[2], m.r_adj.at[2])
-    share = channels // n_rep
     pick = (lax.broadcasted_iota(jnp.int32, (channels, share), 0)
             == lax.broadcasted_iota(jnp.int32, (channels, share), 1) + r * share).astype(BF16)
     cols = mm(m.slope[...].reshape(atoms, channels), pick).astype(BF16)
     m.mix[...] = tn(m.packed[...].reshape(atoms, channels), cols).reshape(m.mix.shape)
-    for slot, j in ((1, 2 + 2 * c), (2, 3 + 2 * c), (0, c)):
-        take(m.gp.at[slot], m.s_gp.at[slot], m.r_gp.at[slot])
+    for slot, j in held:
         take(m.gs.at[slot], m.s_gs.at[slot], m.r_gs.at[slot])
-        m.sb[slot] = (m.gfeat[j].astype(F32) + m.gp[slot].astype(F32)).astype(BF16)
         m.ss[slot] = m.side[j] + m.gs[slot]
         for half in ((0, 1) if slot else (1 - y,)):
             dest = at(dom_at(-mine[slot - 1]) if slot else d, 2 * half + c)
-            push(m.sb.at[slot, half], m.rf.at[slot, y], m.s_rf.at[slot, half], m.r_rf.at[slot, y], dest)
             push(m.ss.at[slot], m.rs.at[slot, y], m.s_rs.at[slot, half], m.r_rs.at[slot, y], dest)
 
     def mix_copy(i):
@@ -349,31 +390,32 @@
                                             device_id=at(to, r), device_id_type=MESH)
 
     lax.fori_loop(1, n_dom, lambda i, _: (mix_copy(i).start(), 0)[1], 0)
-    take(m.rf.at[0, 1 - y], m.s_rf.at[0, 0], m.r_rf.at[0, 1 - y])
+    for q in peers:
+        take(m.ro.at[lax.rem(q, 2), lax.div(q, 2)], m.s_ro.at[0], m.r_ro.at[lax.rem(q, 2), lax.div(q, 2)])
+    total = jnp.concatenate([m.ro[j, 0].astype(F32) + m.ro[j, 1].astype(F32) for j in range(own)], axis=1)
+    for t in range(4):
+        hot = (iota == m.rows[t:t + 1, :]).astype(F32).astype(BF16)
+        for s in range(2):
+            take(m.rf.at[t, s], m.s_rf.at[0, 0], m.r_rf.at[t, s])
+        both = nt(m.rf[t].reshape(2 * share, TILE), hot)
+        total = total + (both[:share] + both[share:])
+    m.part[r] = total.astype(BF16)
+    for i, q in enumerate(peers):
+        push(m.part.at[r], m.part.at[r], m.s_part.at[i], m.r_part.at[r], at(d, q))
     take(m.rs.at[0, 1 - y], m.s_rs.at[0, 0], m.r_rs.at[0, 1 - y])
-    feat_self = m.sb[0, y].astype(F32) + m.rf[0, 1 - y].astype(F32)
     side_self = m.ss[0] + m.rs[0, 1 - y]
     is_low = c == 0
-    zero = jnp.zeros_like(feat_self)
-    total = jnp.concatenate([jnp.where(is_low, feat_self, zero), jnp.where(is_low, zero, feat_self)], axis=0)
     zside = jnp.zeros_like(side_self)
     total_side = jnp.concatenate([jnp.where(is_low, side_self, zside), jnp.where(is_low, zside, side_self)],
                                  axis=1)
     for q in range(2):
         hot = (iota == m.rows[pl.ds(2 * c + q, 1), :]).astype(F32).astype(BF16)
         slot = 1 + q
-        got = None
         for s in range(2):
-            take(m.rf.at[slot, s], m.s_rf.at[0, 0], m.r_rf.at[slot, s])
             take(m.rs.at[slot, s], m.s_rs.at[0, 0], m.r_rs.at[slot, s])
-            total = total + mm(hot, m.rf[slot, s])
-            got = m.rs[slot, s] if got is None else got + m.rs[slot, s]
-        for v in split3(got):
+        for v in split3(m.rs[slot, 0] + m.rs[slot, 1]):
             total_side = total_side + nt(v, hot)
-    m.part[r] = total.astype(BF16)
     m.pside[...] = total_side
-    for i, q in enumerate(peers):
-        push(m.part.at[r], m.part.at[r], m.s_part.at[i], m.r_part.at[r], at(d, q))
     push(m.pside, m.qside, m.s_side, m.r_side, at(d, partner))
 
     def mix_add(i, value):
@@ -388,9 +430,7 @@
     m.out_virial[...] = final[8:14]
     for q in peers:
         take(m.part.at[q], m.s_part.at[0], m.r_part.at[q])
-    for half in range(2):
-        m.out_feat[:, half * TILE:(half + 1) * TILE] = (
-            m.part[2 * half].astype(F32) + m.part[2 * half + 1].astype(F32)).astype(BF16)
+    m.out_feat[...] = nt(m.eye[:atoms, :atoms], m.part[...].reshape(channels, atoms)).astype(BF16)
     for copy in started:
         copy.wait_send()
     lax.fori_loop(1, n_dom, lambda i, _: (mix_copy(i).wait_send(), 0)[1], 0)
@@ -414,7 +454,7 @@
     pairs = pair_home.shape[0]
     dma = pltpu.SemaphoreType.DMA
     mix_rows, mix_cols = channels // n_dom, channels // n_rep
-    half = (2, TILE, channels // 2)
+    quarters = (n_rep, channels // n_rep, TILE)
     readout_row = readout.reshape(1, channels)
     pair_rows = [a.reshape(1, pairs) for a in (pair_home, pair_other, pair_kind)]
 
@@ -442,18 +482,20 @@
         "adjoint": pltpu.VMEM((own, TILE, channels), BF16), "slope": pltpu.VMEM((own, TILE, channels), BF16),
         "packed": pltpu.VMEM((own, TILE, channels), BF16),
         "weights": pltpu.VMEM((own * kinds, TILE, channels), BF16),
-        "gfeat": pltpu.VMEM((n_ext, *half), BF16), "side": pltpu.VMEM((n_ext, 16, TILE), F32),
-        "gp": pltpu.VMEM((3, *half), BF16), "gs": pltpu.VMEM((3, 16, TILE), F32),
-        "sb": pltpu.VMEM((3, *half), BF16), "ss": pltpu.VMEM((3, 16, TILE), F32),
-        "rf": pltpu.VMEM((3, *half), BF16), "rs": pltpu.VMEM((3, 2, 16, TILE), F32),
+        "gfeat": pltpu.VMEM((n_ext, *quarters), BF16), "side": pltpu.VMEM((n_ext, 16, TILE), F32),
+        "gp": pltpu.VMEM((3, *quarters), BF16), "gs": pltpu.VMEM((3, 16, TILE), F32),
+        "sb": pltpu.VMEM((3, *quarters), BF16), "ss": pltpu.VMEM((3, 16, TILE), F32),
+        "rf": pltpu.VMEM((4, 2, *quarters[1:]), BF16), "ro": pltpu.VMEM((own, 2, *quarters[1:]), BF16), "rs": pltpu.VMEM((3, 2, 16, TILE), F32),
         "mix": pltpu.VMEM((n_dom, mix_rows, mix_cols), F32), "rm": pltpu.VMEM((n_dom, mix_rows, mix_cols), F32),
-        "part": pltpu.VMEM((n_rep, atoms, channels // 2), BF16),
+        "part": pltpu.VMEM((n_rep, channels // n_rep, atoms), BF16),
+        "eye": pltpu.VMEM((max(atoms, channels),) * 2, BF16),
         "pside": pltpu.VMEM((16, atoms), F32), "qside": pltpu.VMEM((16, atoms), F32),
         "load": dma((len(INPUTS),)), "s_plan": dma, "s_pos": dma((2, 2)), "r_pos": dma((4,)),
         "s_feat": dma((2,)), "r_feat": dma((4,)), "s_relay": dma((2,)), "r_relay": dma((4,)),
         "s_msg": dma((2,)), "r_msg": dma((2,)), "s_adj": dma((3,)), "r_adj": dma((3,)),
         "s_gp": dma((3,)), "r_gp": dma((3,)), "s_gs": dma((3,)), "r_gs": dma((3,)),
-        "s_rf": dma((3, 2)), "r_rf": dma((3, 2)), "s_rs": dma((3, 2)), "r_rs": dma((3, 2)),
+        "s_rf": dma((2, n_rep)), "r_rf": dma((4, 2)),
+        "s_ro": dma((n_rep,)), "r_ro": dma((own, 2)), "s_rs": dma((3, 2)), "r_rs": dma((3, 2)),
         "s_mix": dma((n_dom,)), "r_mix": dma((n_dom,)), "s_part": dma((n_rep,)), "r_part": dma((n_rep,)),
         "s_side": dma, "r_side": dma,
     }

time: 39.5 us -> 37 us (0.937)
  Pallas kernels: 38.6 us -> 36.2 us
    pallas_call x1, Pallas kernels: 37.9 us -> 35.5 us  [on_device(): pl.pallas_call(functools.partial(kernel, INPUTS + OUTPUTS + tuple(scratch...]
where the time goes in v2:
time: 37 us; the launch traced here: 36.8 us
  Pallas kernels  36.2 us (98%)
  between operations  0.64 us (2%)
    pallas_call x1, Pallas kernels, on_device(): pl.pallas_call(functools.partial(kernel, INPUTS + OUTPUTS + tuple(scratch...  35.5 us

profile of v2, /device:TPU:0, one launch (start us, length us, event | category | flops | bytes accessed | tf_op | source)
XLA Modules:
  0.0 36.8 jit_solution(11333035164170995843)
XLA Ops:
  0.6 35.5 %layer.1 = (bf16[256,256]{1,0:T(8,128)(2,1)S(1)}, f32[3,256]{1,0:T(4,128)S(1)}, f32[6,256]{1,0:T(8,128)S(1)}, f32[32,64]{1,0:T(8,128)S(1)}) custom-call(bf16[256,256]{1,0:T(8,128)(2,1)} %refs_0_.1, f32[3,256]{1,0:T(4,128)} %refs_1_.1, s32[4,128]{1,0:T(4,128)} %refs_2_.1, bf16[8,256,256]{2,1,0:T(8,128)(2,1)} %refs_3_.1, bf16[256,256]{1,0:T(8,128)(2,1)} %refs_4_.1, ...), custom_call_target="tpu_custom_call" | custom-call | tf_op jit(solution)/shard_map/layer/pallas_call | solution.py:506
  36.1 0.7 %copy_out.1 = (bf16[256,256]{1,0:T(8,128)(2,1)}, f32[3,256]{1,0:T(4,128)}, f32[6,256]{1,0:T(8,128)}, f32[32,64]{1,0:T(8,128)}) custom-call(bf16[256,256]{1,0:T(8,128)(2,1)S(1)} %get-tuple-element.8.a, f32[3,256]{1,0:T(4,128)S(1)} %get-tuple-element.9.b, f32[6,256]{1,0:T(8,128)S(1)} %get-tuple-element.10.c, f32[32,64]{1,0:T(8,128)S(1)} %get-tuple-element.11.d), custom_call_target="tpu_custom_call" | custom-call | tf_op jit(solution)/shard_map/copy_out/pallas_call | solution.py:518

commit v3 on v2

--- a/solution.py
+++ b/solution.py
@@ -12,9 +12,9 @@
 OFFSETS = (1, -1, 2, -2)
 CELL = 2.0
 GROUP = 4
-FORWARD_GROUP = 8
+WIDE_GROUP = 24
 BACK_GROUP = 12
-SPREAD_GROUP = 8
+LOG2E = 1.4426950408889634
 F32 = jnp.float32
 BF16 = jnp.bfloat16
 MESH = pl.DeviceIdType.MESH
@@ -68,6 +68,7 @@
     across = r + 2 - 4 * y
     atoms, channels = m.feat.shape
     own = atoms // TILE
+    late = lax.div(n_dom - 1 - d, n_dom // 2)
     pairs = m.home.shape[0]
     kinds = m.radial.shape[0]
     n_ext = m.tiles.shape[0]
@@ -158,23 +159,29 @@
         m.second[j] = two_rows
         stack = jnp.concatenate([one_rows * two_rows, one_rows, two_rows], axis=0)
         parts = [v.astype(F32) for v in split3(stack)]
-        m.moments[j] = jnp.concatenate(
-            [parts[0], jnp.ones((8, TILE), F32), parts[1], parts[2]], axis=0).astype(BF16)
+        stack = jnp.concatenate([parts[0], jnp.ones((8, TILE), F32), parts[1], parts[2]], axis=0).astype(BF16)
+        m.moments[j] = stack
+        if j < own:
+            m.sided[j, 0] = jnp.concatenate([stack, jnp.zeros_like(stack)], axis=1)
+            m.sided[j, 1] = jnp.concatenate([jnp.zeros_like(stack), stack], axis=1)
 
     for j in range(own):
         m.tiles[j] = m.pos[:, j * TILE:(j + 1) * TILE]
         m.ext[j] = m.feat[j * TILE:(j + 1) * TILE, :]
         columns(j)
     pl.semaphore_wait(barrier, 6 + n_rep - 1 + n_dom - 1)
-    for q in range(2):
+    for q in (late, 1 - late):
         for i, rep in enumerate((r, partner)):
             push(m.sendp.at[q], m.recvp.at[2 * c + q], m.s_pos.at[q, i], m.r_pos.at[2 * c + q],
-                 at(dom_at(mine[q]), rep))
-    for q in range(2):
+                 at(dom_at((c + 1) * (1 - 2 * q)), rep))
+    for q in (late, 1 - late):
         push(m.sendf.at[q], m.ext.at[own + 2 * c + q], m.s_feat.at[q], m.r_feat.at[2 * c + q],
-             at(dom_at(mine[q]), r))
+             at(dom_at((c + 1) * (1 - 2 * q)), r))
 
     m.sums[0] = jnp.zeros_like(m.sums[0])
+    m.carry[...] = jnp.zeros_like(m.carry)
+    for t in range(4):
+        m.hot[:, t * TILE:(t + 1) * TILE] = (iota == m.rows[t:t + 1, :]).astype(F32).astype(BF16)
     m.far[0] = jnp.zeros_like(m.far[0])
     m.near[...] = jnp.zeros_like(m.near)
     m.eye[...] = (lax.broadcasted_iota(jnp.int32, m.eye.shape, 0)
@@ -196,7 +203,7 @@
             for x in range(3):
                 sep = (row[x:x + 1, :] + m.image[x, p].astype(F32) * CELL) - m.col[h, x]
                 d2 = sep * sep if d2 is None else d2 + sep * sep
-            m.kern_ab[p] = jnp.exp(d2 * (-m.decay[k])).astype(BF16)
+            m.kern_ab[p] = jnp.exp2(d2 * (-LOG2E * m.decay[k])).astype(BF16)
         return 0
 
     def transposed(g, _):
@@ -208,7 +215,7 @@
             for x in range(3):
                 sep = m.col[o, x] - (row[x:x + 1, :] - m.image[x, p].astype(F32) * CELL)
                 d2 = sep * sep if d2 is None else d2 + sep * sep
-            m.kern_ba[p] = jnp.exp(d2 * (-m.decay[k]))
+            m.kern_ba[p] = jnp.exp2(d2 * (-LOG2E * m.decay[k]))
         return 0
 
     half_steps = pairs // GROUP // 2
@@ -233,53 +240,56 @@
         return m.home[p] * kinds + m.kind[p]
 
     def forward(g, _):
-        acc = m.sums[g * FORWARD_GROUP]
-        for u in range(FORWARD_GROUP):
-            i = g * FORWARD_GROUP + u
+        acc = m.carry[...]
+        for u in range(WIDE_GROUP):
+            i = g * WIDE_GROUP + u
             p = pair_at(0, i)
             last = pair_at(0, jnp.maximum(i - 1, 0))
             keep = (seg_f(p) == seg_f(last)).astype(F32)
             acc = acc * keep + mm(m.kern_ab[p], m.ext[m.other[p]])
-            m.sums[i + 1] = acc
+            m.sums[i + 1] = acc.astype(BF16)
+        m.carry[...] = acc
         return 0
 
-    lax.fori_loop(0, pairs // FORWARD_GROUP, forward, 0)
+    lax.fori_loop(0, pairs // WIDE_GROUP, forward, 0)
 
     def message(h):
-        left = [m.sums[sum_at(2, h * kinds + k)].astype(BF16) for k in range(kinds)]
+        left = [m.sums[sum_at(2, h * kinds + k)] for k in range(kinds)]
         return mm(jnp.concatenate(left, axis=1), m.radial[...].reshape(kinds * channels, channels))
 
-    m.msg[...] = message(mate).astype(BF16)
-    push(m.msg, m.msg_in, m.s_msg.at[0], m.r_msg.at[0], at(d, partner))
-    value = message(c)
+    m.msg[...] = message(mate).astype(BF16).reshape(m.msg.shape)
+    for q in range(2):
+        push(m.msg.at[q], m.msg_in.at[q], m.s_msg.at[q], m.r_msg.at[q], at(d, partner))
+    value = message(c).reshape(m.msg.shape)
     for t in range(4):
         columns(own + t)
         table(own + t)
-    take(m.msg_in, m.s_msg.at[0], m.r_msg.at[0])
-    value = (value + m.msg_in[...].astype(F32)).astype(BF16)
-    m.chip[...] = value
-    push(m.chip, m.chip_in, m.s_msg.at[1], m.r_msg.at[1], at(d, across))
+    for q in range(2):
+        take(m.msg_in.at[q], m.s_msg.at[q], m.r_msg.at[q])
+        m.chip[q] = (value[q] + m.msg_in[q].astype(F32)).astype(BF16)
+        push(m.chip.at[q], m.chip_in.at[q], m.s_chip.at[q], m.r_chip.at[q], at(d, across))
     lax.fori_loop(0, pairs // GROUP, transposed, 0)
-    take(m.chip_in, m.s_msg.at[1], m.r_msg.at[1])
-    low = (value.astype(F32) + m.chip_in[...].astype(F32)).astype(BF16)
-    mixed = mm(low, m.mixing[...])
-    sig = jax.nn.sigmoid(mixed)
-    slope = (m.readout[...] * sig * (1.0 + mixed * (1.0 - sig))).astype(BF16)
-    adj = nt(slope, m.mixing[...]).astype(BF16)
-    m.adjoint[c] = adj
-    push(m.adjoint.at[c], m.adjoint.at[c], m.s_adj.at[0], m.r_adj.at[0], at(d, partner))
-    m.slope[c] = slope
-    push(m.slope.at[c], m.slope.at[c], m.s_adj.at[1], m.r_adj.at[1], at(d, partner))
-    m.packed[c] = low
-    push(m.packed.at[c], m.packed.at[c], m.s_adj.at[2], m.r_adj.at[2], at(d, partner))
+    for q in range(2):
+        take(m.chip_in.at[q], m.s_chip.at[q], m.r_chip.at[q])
+        low = (m.chip[q].astype(F32) + m.chip_in[q].astype(F32)).astype(BF16)
+        mixed = mm(low, m.mixing[...])
+        sig = jax.nn.sigmoid(mixed)
+        slope = (m.readout[...] * sig * (1.0 + mixed * (1.0 - sig))).astype(BF16)
+        m.adjoint[c, q] = nt(slope, m.mixing[...]).astype(BF16)
+        push(m.adjoint.at[c, q], m.adjoint.at[c, q], m.s_adj.at[q], m.r_adj.at[q], at(d, partner))
+        m.slope[c, q] = slope
+        m.packed[c, q] = low
+    push(m.slope.at[c], m.slope.at[c], m.s_adj.at[2], m.r_adj.at[2], at(d, partner))
+    push(m.packed.at[c], m.packed.at[c], m.s_adj.at[3], m.r_adj.at[3], at(d, partner))
 
     def spread(h):
-        value = m.adjoint[h]
+        value = m.adjoint[h].reshape(TILE, channels)
         for k in range(kinds):
             m.weights[h * kinds + k] = nt(value, m.radial[k]).astype(BF16)
 
     spread(c)
-    take(m.adjoint.at[mate], m.s_adj.at[0], m.r_adj.at[0])
+    for q in range(2):
+        take(m.adjoint.at[mate, q], m.s_adj.at[q], m.r_adj.at[q])
     spread(mate)
 
     sub = lax.broadcasted_iota(jnp.int32, (8, TILE), 0)
@@ -302,12 +312,13 @@
         return p, m.home[p], m.other[p], m.kind[p], keep
 
     def spread_back(g, _):
-        acc = m.sums[g * SPREAD_GROUP]
-        for u in range(SPREAD_GROUP):
-            i = g * SPREAD_GROUP + u
+        acc = m.carry[...]
+        for u in range(WIDE_GROUP):
+            i = g * WIDE_GROUP + u
             p, h, _, k, keep = pair_b(i)
             acc = acc * keep + mm(m.kern_ba[p].astype(BF16), m.weights[h * kinds + k])
-            m.sums[i + 1] = acc
+            m.sums[i + 1] = acc.astype(BF16)
+        m.carry[...] = acc
         return 0
 
     def backward(g, _):
@@ -319,12 +330,19 @@
             found.append((i, p, h, o, keep, ((-2.0 * m.decay[k]) * m.kern_ba[p] * grad).astype(BF16)))
         far = m.far[g * BACK_GROUP]
         near = [m.near[j] for j in range(own)]
-        for i, p, h, o, keep, weight in found:
+        results = []
+        for one, two in zip(found[::2], found[1::2]):
+            weight = jnp.concatenate([one[-1], two[-1]], axis=1)
+            close = mm(jnp.concatenate([m.moments[one[3]], m.moments[two[3]]], axis=0), weight)
+            beyond = nt(jnp.concatenate([m.sided[one[2], 0], m.sided[two[2], 1]], axis=0), weight)
+            size = close.shape[0] // 2
+            results += [(close[:size, :TILE], beyond[:size]), (close[size:, TILE:], beyond[size:])]
+        for (i, p, h, o, keep, _), (close, beyond) in zip(found, results):
             shift = [m.image[x, p].astype(F32) * CELL for x in range(3)]
             s1 = jnp.where(is_x1, shift[0], jnp.where(is_y1, shift[1], shift[2]))
             s2 = jnp.where(is_x2, shift[0], jnp.where(is_y2, shift[1], shift[2]))
-            near_side = combine(mm(m.moments[o], weight), m.first[h] - s1, m.second[h] - s2)
-            far_side = combine(nt(m.moments[h], weight), m.first[o] + s1, m.second[o] + s2)
+            near_side = combine(close, m.first[h] - s1, m.second[h] - s2)
+            far_side = combine(beyond, m.first[o] + s1, m.second[o] + s2)
             for j in range(own):
                 near[j] = near[j] + near_side * (h == j).astype(F32)
             far = far * keep + far_side
@@ -333,57 +351,46 @@
             m.near[j] = near[j]
         return 0
 
-    lax.fori_loop(0, pairs // SPREAD_GROUP, spread_back, 0)
+    m.carry[...] = jnp.zeros_like(m.carry)
+    lax.fori_loop(0, pairs // WIDE_GROUP, spread_back, 0)
 
     share = channels // n_rep
-    away = ((1, 2 + 2 * mate), (2, 3 + 2 * mate), (0, mate))
-    held = ((1, 2 + 2 * c), (2, 3 + 2 * c), (0, c))
-
-    def settle(slots):
-        total = jnp.concatenate([m.sums[sum_at(3, j)].astype(BF16) for _, j in slots], axis=0)
+    slots = (2 - late, 1 + late, 0)
+    away = [(slot, own + 2 * mate + slot - 1) for slot in slots[:2]] + [(0, mate)]
+    held = [(slot, own + 2 * c + slot - 1) for slot in slots[:2]] + [(0, c)]
+
+    def settle(group):
+        total = jnp.concatenate([m.sums[sum_at(3, j)] for _, j in group], axis=0)
         turned = nt(m.eye[:channels, :channels], total).astype(BF16)
-        for i, (_, j) in enumerate(slots):
+        for i, (_, j) in enumerate(group):
             m.gfeat[j] = turned[:, i * TILE:(i + 1) * TILE].reshape(n_rep, share, TILE)
 
     settle(away)
     for slot, j in away:
         push(m.gfeat.at[j], m.gp.at[slot], m.s_gp.at[slot], m.r_gp.at[slot], at(d, partner))
     settle(held)
-    half_back = pairs // BACK_GROUP // 2
-    lax.fori_loop(0, half_back, backward, 0)
-    for slot, j in held:
+    lax.fori_loop(0, 1, backward, 0)
+    for place, (slot, j) in enumerate(held):
         take(m.gp.at[slot], m.s_gp.at[slot], m.r_gp.at[slot])
         m.sb[slot] = (m.gfeat[j].astype(F32) + m.gp[slot].astype(F32)).astype(BF16)
-        if slot:
+        if place < 2:
             t = 2 * c + slot - 1
             for q in range(n_rep):
                 push(m.sb.at[slot, q], m.rf.at[t, y], m.s_rf.at[slot - 1, q], m.r_rf.at[t, y],
-                     at(dom_at(-mine[slot - 1]), q))
+                     at(dom_at((c + 1) * (2 * slot - 3)), q))
     for i, q in enumerate(peers):
         push(m.sb.at[0, q], m.ro.at[c, y], m.s_ro.at[i], m.r_ro.at[c, y], at(d, q))
     m.ro[c, y] = m.sb[0, r]
-    lax.fori_loop(half_back, pairs // BACK_GROUP, backward, 0)
-    def settle_side(slot, j):
-        m.side[j] = m.far[sum_at(3, j)] if slot else m.far[sum_at(3, j)] + m.near[j]
-
-    for slot, j in away:
-        settle_side(slot, j)
-        push(m.side.at[j], m.gs.at[slot], m.s_gs.at[slot], m.r_gs.at[slot], at(d, partner))
-    for slot, j in held:
-        settle_side(slot, j)
-    take(m.slope.at[mate], m.s_adj.at[1], m.r_adj.at[1])
-    take(m.packed.at[mate], m.s_adj.at[2], m.r_adj.at[2])
+    lax.fori_loop(1, pairs // BACK_GROUP, backward, 0)
+    for t, o in enumerate(OFFSETS):
+        m.side[t] = m.far[sum_at(3, own + t)]
+        push(m.side.at[t], m.rs.at[t], m.s_rs.at[t], m.r_rs.at[t], at(dom_at(-o), r))
+    take(m.slope.at[mate], m.s_adj.at[2], m.r_adj.at[2])
+    take(m.packed.at[mate], m.s_adj.at[3], m.r_adj.at[3])
     pick = (lax.broadcasted_iota(jnp.int32, (channels, share), 0)
             == lax.broadcasted_iota(jnp.int32, (channels, share), 1) + r * share).astype(BF16)
     cols = mm(m.slope[...].reshape(atoms, channels), pick).astype(BF16)
     m.mix[...] = tn(m.packed[...].reshape(atoms, channels), cols).reshape(m.mix.shape)
-    for slot, j in held:
-        take(m.gs.at[slot], m.s_gs.at[slot], m.r_gs.at[slot])
-        m.ss[slot] = m.side[j] + m.gs[slot]
-        for half in ((0, 1) if slot else (1 - y,)):
-            dest = at(dom_at(-mine[slot - 1]) if slot else d, 2 * half + c)
-            push(m.ss.at[slot], m.rs.at[slot, y], m.s_rs.at[slot, half], m.r_rs.at[slot, y], dest)
-
     def mix_copy(i):
         to = lax.rem(d + i, n_dom)
         return pltpu.make_async_remote_copy(m.mix.at[to], m.rm.at[d], m.s_mix.at[i], m.r_mix.at[d],
@@ -394,29 +401,20 @@
         take(m.ro.at[lax.rem(q, 2), lax.div(q, 2)], m.s_ro.at[0], m.r_ro.at[lax.rem(q, 2), lax.div(q, 2)])
     total = jnp.concatenate([m.ro[j, 0].astype(F32) + m.ro[j, 1].astype(F32) for j in range(own)], axis=1)
     for t in range(4):
-        hot = (iota == m.rows[t:t + 1, :]).astype(F32).astype(BF16)
-        for s in range(2):
-            take(m.rf.at[t, s], m.s_rf.at[0, 0], m.r_rf.at[t, s])
-        both = nt(m.rf[t].reshape(2 * share, TILE), hot)
-        total = total + (both[:share] + both[share:])
-    m.part[r] = total.astype(BF16)
+        for q in range(2):
+            take(m.rf.at[t, q], m.s_rf.at[0, 0], m.r_rf.at[t, q])
+    both = nt(jnp.concatenate([m.rf[t].reshape(2 * share, TILE) for t in range(4)], axis=1), m.hot[...])
+    m.part[r] = (total + (both[:share] + both[share:])).astype(BF16)
     for i, q in enumerate(peers):
         push(m.part.at[r], m.part.at[r], m.s_part.at[i], m.r_part.at[r], at(d, q))
-    take(m.rs.at[0, 1 - y], m.s_rs.at[0, 0], m.r_rs.at[0, 1 - y])
-    side_self = m.ss[0] + m.rs[0, 1 - y]
-    is_low = c == 0
-    zside = jnp.zeros_like(side_self)
-    total_side = jnp.concatenate([jnp.where(is_low, side_self, zside), jnp.where(is_low, zside, side_self)],
-                                 axis=1)
-    for q in range(2):
-        hot = (iota == m.rows[pl.ds(2 * c + q, 1), :]).astype(F32).astype(BF16)
-        slot = 1 + q
-        for s in range(2):
-            take(m.rs.at[slot, s], m.s_rs.at[0, 0], m.r_rs.at[slot, s])
-        for v in split3(m.rs[slot, 0] + m.rs[slot, 1]):
-            total_side = total_side + nt(v, hot)
-    m.pside[...] = total_side
-    push(m.pside, m.qside, m.s_side, m.r_side, at(d, partner))
+    for t in range(4):
+        take(m.rs.at[t], m.s_rs.at[t], m.r_rs.at[t])
+    left = jnp.concatenate([jnp.concatenate(split3(m.rs[t]), axis=0) for t in range(4)], axis=1)
+    spots = nt(left, m.hot[...])
+    m.pside[r] = (jnp.concatenate([m.far[sum_at(3, j)] + m.near[j] for j in range(own)], axis=1)
+                  + (spots[0:16] + spots[16:32] + spots[32:48]))
+    for i, q in enumerate(peers):
+        push(m.pside.at[r], m.pside.at[r], m.s_side.at[i], m.r_side.at[r], at(d, q))
 
     def mix_add(i, value):
         frm = lax.rem(d + i, n_dom)
@@ -424,8 +422,9 @@
         return value + m.rm[frm]
 
     m.out_mix[...] = lax.fori_loop(1, n_dom, mix_add, m.mix[d])
-    take(m.qside, m.s_side, m.r_side)
-    final = total_side + m.qside[...]
+    for q in peers:
+        take(m.pside.at[q], m.s_side.at[0], m.r_side.at[q])
+    final = (m.pside[0] + m.pside[1]) + (m.pside[2] + m.pside[3])
     m.out_force[...] = final[0:3]
     m.out_virial[...] = final[8:14]
     for q in peers:
@@ -473,31 +472,33 @@
         "recvp": pltpu.VMEM((4, 3, TILE), F32), "ext": pltpu.VMEM((n_ext, TILE, channels), BF16),
         "tiles": pltpu.VMEM((n_ext, 3, TILE), F32), "col": pltpu.VMEM((n_ext, 3, TILE, TILE), F32),
         "moments": pltpu.VMEM((n_ext, 80, TILE), BF16),
+        "sided": pltpu.VMEM((own, 2, 80, 2 * TILE), BF16), "hot": pltpu.VMEM((atoms, 4 * TILE), BF16),
         "first": pltpu.VMEM((n_ext, 8, TILE), F32), "second": pltpu.VMEM((n_ext, 8, TILE), F32),
         "kern_ab": pltpu.VMEM((pairs, TILE, TILE), BF16), "kern_ba": pltpu.VMEM((pairs, TILE, TILE), F32),
-        "sums": pltpu.VMEM((pairs + 1, TILE, channels), F32), "far": pltpu.VMEM((pairs + 1, 16, TILE), F32),
+        "sums": pltpu.VMEM((pairs + 1, TILE, channels), BF16),
+        "carry": pltpu.VMEM((TILE, channels), F32), "far": pltpu.VMEM((pairs + 1, 16, TILE), F32),
         "near": pltpu.VMEM((own, 16, TILE), F32),
-        "msg": pltpu.VMEM((TILE, channels), BF16), "msg_in": pltpu.VMEM((TILE, channels), BF16),
-        "chip": pltpu.VMEM((TILE, channels), BF16), "chip_in": pltpu.VMEM((TILE, channels), BF16),
-        "adjoint": pltpu.VMEM((own, TILE, channels), BF16), "slope": pltpu.VMEM((own, TILE, channels), BF16),
-        "packed": pltpu.VMEM((own, TILE, channels), BF16),
+        "msg": pltpu.VMEM((2, TILE // 2, channels), BF16), "msg_in": pltpu.VMEM((2, TILE // 2, channels), BF16),
+        "chip": pltpu.VMEM((2, TILE // 2, channels), BF16), "chip_in": pltpu.VMEM((2, TILE // 2, channels), BF16),
+        "adjoint": pltpu.VMEM((own, 2, TILE // 2, channels), BF16), "slope": pltpu.VMEM((own, 2, TILE // 2, channels), BF16),
+        "packed": pltpu.VMEM((own, 2, TILE // 2, channels), BF16),
         "weights": pltpu.VMEM((own * kinds, TILE, channels), BF16),
-        "gfeat": pltpu.VMEM((n_ext, *quarters), BF16), "side": pltpu.VMEM((n_ext, 16, TILE), F32),
-        "gp": pltpu.VMEM((3, *quarters), BF16), "gs": pltpu.VMEM((3, 16, TILE), F32),
-        "sb": pltpu.VMEM((3, *quarters), BF16), "ss": pltpu.VMEM((3, 16, TILE), F32),
-        "rf": pltpu.VMEM((4, 2, *quarters[1:]), BF16), "ro": pltpu.VMEM((own, 2, *quarters[1:]), BF16), "rs": pltpu.VMEM((3, 2, 16, TILE), F32),
+        "gfeat": pltpu.VMEM((n_ext, *quarters), BF16), "side": pltpu.VMEM((4, 16, TILE), F32),
+        "gp": pltpu.VMEM((3, *quarters), BF16),
+        "sb": pltpu.VMEM((3, *quarters), BF16),
+        "rf": pltpu.VMEM((4, 2, *quarters[1:]), BF16), "ro": pltpu.VMEM((own, 2, *quarters[1:]), BF16), "rs": pltpu.VMEM((4, 16, TILE), F32),
         "mix": pltpu.VMEM((n_dom, mix_rows, mix_cols), F32), "rm": pltpu.VMEM((n_dom, mix_rows, mix_cols), F32),
         "part": pltpu.VMEM((n_rep, channels // n_rep, atoms), BF16),
         "eye": pltpu.VMEM((max(atoms, channels),) * 2, BF16),
-        "pside": pltpu.VMEM((16, atoms), F32), "qside": pltpu.VMEM((16, atoms), F32),
+        "pside": pltpu.VMEM((n_rep, 16, atoms), F32),
         "load": dma((len(INPUTS),)), "s_plan": dma, "s_pos": dma((2, 2)), "r_pos": dma((4,)),
         "s_feat": dma((2,)), "r_feat": dma((4,)), "s_relay": dma((2,)), "r_relay": dma((4,)),
-        "s_msg": dma((2,)), "r_msg": dma((2,)), "s_adj": dma((3,)), "r_adj": dma((3,)),
-        "s_gp": dma((3,)), "r_gp": dma((3,)), "s_gs": dma((3,)), "r_gs": dma((3,)),
+        "s_msg": dma((2,)), "r_msg": dma((2,)), "s_chip": dma((2,)), "r_chip": dma((2,)), "s_adj": dma((4,)), "r_adj": dma((4,)),
+        "s_gp": dma((3,)), "r_gp": dma((3,)),
         "s_rf": dma((2, n_rep)), "r_rf": dma((4, 2)),
-        "s_ro": dma((n_rep,)), "r_ro": dma((own, 2)), "s_rs": dma((3, 2)), "r_rs": dma((3, 2)),
+        "s_ro": dma((n_rep,)), "r_ro": dma((own, 2)), "s_rs": dma((4,)), "r_rs": dma((4,)),
         "s_mix": dma((n_dom,)), "r_mix": dma((n_dom,)), "s_part": dma((n_rep,)), "r_part": dma((n_rep,)),
-        "s_side": dma, "r_side": dma,
+        "s_side": dma((n_rep,)), "r_side": dma((n_rep,)),
     }
 
     def shape(dims, dtype):

time: 37 us -> 35.5 us (0.959)
  Pallas kernels: 36.2 us -> 34.7 us
    pallas_call x1, Pallas kernels: 35.5 us -> 34 us  [on_device(): pl.pallas_call(functools.partial(kernel, INPUTS + OUTPUTS + tuple(scratch...]
where the time goes in v3:
time: 35.5 us; the launch traced here: 35.3 us
  Pallas kernels  34.7 us (98%)
  between operations  0.64 us (2%)
    pallas_call x1, Pallas kernels, on_device(): pl.pallas_call(functools.partial(kernel, INPUTS + OUTPUTS + tuple(scratch...  34 us

profile of v3, /device:TPU:0, one launch (start us, length us, event | category | flops | bytes accessed | tf_op | source)
XLA Modules:
  0.0 35.3 jit_solution(12782337523997170654)
XLA Ops:
  0.6 34.0 %layer.1 = (bf16[256,256]{1,0:T(8,128)(2,1)S(1)}, f32[3,256]{1,0:T(4,128)S(1)}, f32[6,256]{1,0:T(8,128)S(1)}, f32[32,64]{1,0:T(8,128)S(1)}) custom-call(bf16[256,256]{1,0:T(8,128)(2,1)} %refs_0_.1, f32[3,256]{1,0:T(4,128)} %refs_1_.1, s32[4,128]{1,0:T(4,128)} %refs_2_.1, bf16[8,256,256]{2,1,0:T(8,128)(2,1)} %refs_3_.1, bf16[256,256]{1,0:T(8,128)(2,1)} %refs_4_.1, ...), custom_call_target="tpu_custom_call" | custom-call | tf_op jit(solution)/shard_map/layer/pallas_call | solution.py:507
  34.6 0.7 %copy_out.1 = (bf16[256,256]{1,0:T(8,128)(2,1)}, f32[3,256]{1,0:T(4,128)}, f32[6,256]{1,0:T(8,128)}, f32[32,64]{1,0:T(8,128)}) custom-call(bf16[256,256]{1,0:T(8,128)(2,1)S(1)} %get-tuple-element.8.a, f32[3,256]{1,0:T(4,128)S(1)} %get-tuple-element.9.b, f32[6,256]{1,0:T(8,128)S(1)} %get-tuple-element.10.c, f32[32,64]{1,0:T(8,128)S(1)} %get-tuple-element.11.d), custom_call_target="tpu_custom_call" | custom-call | tf_op jit(solution)/shard_map/copy_out/pallas_call | solution.py:519

commit v4 on v3

--- a/solution.py
+++ b/solution.py
@@ -79,12 +79,13 @@
     def at(dom, rep):
         return {"dom": dom, "rep": rep}
 
-    loads = [pltpu.make_async_copy(src, dst, m.load.at[i]) for i, (src, dst) in enumerate((
-        (m.rows_h, m.rows), (m.feat_h, m.feat), (m.pos_h, m.pos), (m.home_row_h, m.home_row),
-        (m.other_row_h, m.other_row), (m.kind_row_h, m.kind_row), (m.radial_h, m.radial), (m.decay_h, m.decay),
-        (m.home_h, m.home), (m.other_h, m.other), (m.kind_h, m.kind), (m.image_h, m.image),
-        (m.mixing_h, m.mixing), (m.readout_h, m.readout)))]
-    for copy in loads[:3]:
+    groups = ((m.rows_h, m.rows), (m.feat_h, m.feat), (m.pos_h, m.pos)), (
+        (m.home_row_h, m.home_row), (m.other_row_h, m.other_row), (m.kind_row_h, m.kind_row)), (
+        (m.radial_h, m.radial), (m.decay_h, m.decay), (m.home_h, m.home), (m.other_h, m.other),
+        (m.kind_h, m.kind), (m.image_h, m.image), (m.mixing_h, m.mixing), (m.readout_h, m.readout))
+    loads = [[pltpu.make_async_copy(src, dst, m.load.at[i]) for src, dst in group]
+             for i, group in enumerate(groups)]
+    for copy in loads[0]:
         copy.start()
     barrier = pltpu.get_barrier_semaphore()
     mine = (c + 1, -(c + 1))
@@ -101,25 +102,24 @@
     lax.fori_loop(1, n_dom, greet, 0)
     for o in mine:
         hello(dom_at(o), partner)
-        hello(dom_at(o), across)
     for o in theirs:
         hello(dom_at(o), partner)
     for q in peers:
         hello(d, q)
-    for copy in loads[3:]:
+    for copy in loads[1] + loads[2]:
         copy.start()
 
     started = []
 
-    def push(src, dst, ss, rs, target):
-        copy = pltpu.make_async_remote_copy(src, dst, ss, rs, device_id=target, device_id_type=MESH)
+    def push(src, dst, rs, target):
+        copy = pltpu.make_async_remote_copy(src, dst, m.sent, rs, device_id=target, device_id_type=MESH)
         copy.start()
         started.append(copy)
 
-    def take(dst, ss, rs):
-        pltpu.make_async_remote_copy(dst, dst, ss, rs, device_id=at(d, partner), device_id_type=MESH).wait_recv()
-
-    for copy in loads[:3]:
+    def take(dst, rs):
+        pltpu.make_async_remote_copy(dst, dst, m.sent, rs, device_id=at(d, partner), device_id_type=MESH).wait_recv()
+
+    for copy in loads[0]:
         copy.wait()
     iota = lax.broadcasted_iota(jnp.int32, (atoms, TILE), 0)
     hots = []
@@ -129,7 +129,7 @@
         m.sendp[q] = jnp.dot(m.pos[...], hot, precision=lax.Precision.HIGHEST, preferred_element_type=F32)
     for q in range(2):
         m.sendf[q] = tn(hots[q], m.feat[...]).astype(BF16)
-    for copy in loads[3:6]:
+    for copy in loads[1]:
         copy.wait()
     m.raw[...] = jnp.zeros_like(m.raw)
     for i, src in enumerate((m.home_row, m.kind_row, m.other_row)):
@@ -169,15 +169,17 @@
         m.tiles[j] = m.pos[:, j * TILE:(j + 1) * TILE]
         m.ext[j] = m.feat[j * TILE:(j + 1) * TILE, :]
         columns(j)
-    pl.semaphore_wait(barrier, 6 + n_rep - 1 + n_dom - 1)
+    pl.semaphore_wait(barrier, 4 + n_rep - 1 + n_dom - 1)
     for q in (late, 1 - late):
         for i, rep in enumerate((r, partner)):
-            push(m.sendp.at[q], m.recvp.at[2 * c + q], m.s_pos.at[q, i], m.r_pos.at[2 * c + q],
+            push(m.sendp.at[q], m.recvp.at[2 * c + q], m.r_pos,
                  at(dom_at((c + 1) * (1 - 2 * q)), rep))
     for q in (late, 1 - late):
-        push(m.sendf.at[q], m.ext.at[own + 2 * c + q], m.s_feat.at[q], m.r_feat.at[2 * c + q],
+        push(m.sendf.at[q], m.ext.at[own + 2 * c + q], m.r_feat.at[q],
              at(dom_at((c + 1) * (1 - 2 * q)), r))
 
+    for q in peers:
+        pl.semaphore_signal(m.passed, inc=1, device_id=at(d, q), device_id_type=MESH)
     m.sums[0] = jnp.zeros_like(m.sums[0])
     m.carry[...] = jnp.zeros_like(m.carry)
     for t in range(4):
@@ -188,10 +190,10 @@
                   == lax.broadcasted_iota(jnp.int32, m.eye.shape, 1)).astype(F32).astype(BF16)
     for j in range(own):
         table(j)
-    for copy in loads[6:]:
+    for copy in loads[2]:
         copy.wait()
+    take(m.recvp, m.r_pos)
     for t in range(4):
-        take(m.recvp.at[t], m.s_pos.at[0, 0], m.r_pos.at[t])
         m.tiles[own + t] = m.recvp[t]
 
     def kernels(g, _):
@@ -222,13 +224,11 @@
     lax.fori_loop(0, half_steps, kernels, 0)
     for q in range(2):
         t = 2 * c + q
-        take(m.ext.at[own + t], m.s_feat.at[q], m.r_feat.at[t])
-        push(m.ext.at[own + t], m.ext.at[own + t], m.s_relay.at[q], m.r_relay.at[t], at(d, partner))
+        take(m.ext.at[own + t], m.r_feat.at[q])
+        push(m.ext.at[own + t], m.ext.at[own + t], m.r_relay, at(d, partner))
     lax.fori_loop(half_steps, pairs // GROUP, kernels, 0)
     plan_copy.wait()
-    for q in range(2):
-        t = 2 * mate + q
-        take(m.ext.at[own + t], m.s_relay.at[q], m.r_relay.at[t])
+    take(m.ext.at[pl.ds(own + 2 * mate, 2)], m.r_relay)
 
     def pair_at(row, i):
         return jnp.clip(m.plan[row, i], 0, pairs - 1)
@@ -259,38 +259,35 @@
 
     m.msg[...] = message(mate).astype(BF16).reshape(m.msg.shape)
     for q in range(2):
-        push(m.msg.at[q], m.msg_in.at[q], m.s_msg.at[q], m.r_msg.at[q], at(d, partner))
+        push(m.msg.at[q], m.msg_in.at[q], m.r_msg.at[q], at(d, partner))
     value = message(c).reshape(m.msg.shape)
     for t in range(4):
         columns(own + t)
         table(own + t)
     for q in range(2):
-        take(m.msg_in.at[q], m.s_msg.at[q], m.r_msg.at[q])
+        take(m.msg_in.at[q], m.r_msg.at[q])
         m.chip[q] = (value[q] + m.msg_in[q].astype(F32)).astype(BF16)
-        push(m.chip.at[q], m.chip_in.at[q], m.s_chip.at[q], m.r_chip.at[q], at(d, across))
+        push(m.chip.at[q], m.chip_in.at[q], m.r_chip.at[q], at(d, across))
     lax.fori_loop(0, pairs // GROUP, transposed, 0)
     for q in range(2):
-        take(m.chip_in.at[q], m.s_chip.at[q], m.r_chip.at[q])
+        take(m.chip_in.at[q], m.r_chip.at[q])
         low = (m.chip[q].astype(F32) + m.chip_in[q].astype(F32)).astype(BF16)
         mixed = mm(low, m.mixing[...])
         sig = jax.nn.sigmoid(mixed)
         slope = (m.readout[...] * sig * (1.0 + mixed * (1.0 - sig))).astype(BF16)
         m.adjoint[c, q] = nt(slope, m.mixing[...]).astype(BF16)
-        push(m.adjoint.at[c, q], m.adjoint.at[c, q], m.s_adj.at[q], m.r_adj.at[q], at(d, partner))
-        m.slope[c, q] = slope
-        m.packed[c, q] = low
-    push(m.slope.at[c], m.slope.at[c], m.s_adj.at[2], m.r_adj.at[2], at(d, partner))
-    push(m.packed.at[c], m.packed.at[c], m.s_adj.at[3], m.r_adj.at[3], at(d, partner))
-
-    def spread(h):
-        value = m.adjoint[h].reshape(TILE, channels)
-        for k in range(kinds):
-            m.weights[h * kinds + k] = nt(value, m.radial[k]).astype(BF16)
-
-    spread(c)
-    for q in range(2):
-        take(m.adjoint.at[mate, q], m.s_adj.at[q], m.r_adj.at[q])
-    spread(mate)
+        push(m.adjoint.at[c, q], m.adjoint.at[c, q], m.r_adj, at(d, partner))
+        m.state[0, c, q] = slope
+        m.state[1, c, q] = low
+    push(m.state.at[0, c], m.state.at[0, c], m.r_state, at(d, partner))
+    push(m.state.at[1, c], m.state.at[1, c], m.r_state, at(d, partner))
+
+    take(m.adjoint.at[mate], m.r_adj)
+    adjoint = m.adjoint[...].reshape(atoms, channels)
+    for k in range(kinds):
+        wide = nt(adjoint, m.radial[k]).astype(BF16)
+        for j in range(own):
+            m.weights[j * kinds + k] = wide[j * TILE:(j + 1) * TILE]
 
     sub = lax.broadcasted_iota(jnp.int32, (8, TILE), 0)
     is_x1, is_y1 = (sub == 0) | (sub == 3) | (sub == 4), (sub == 1) | (sub == 5)
@@ -367,68 +364,61 @@
 
     settle(away)
     for slot, j in away:
-        push(m.gfeat.at[j], m.gp.at[slot], m.s_gp.at[slot], m.r_gp.at[slot], at(d, partner))
+        push(m.gfeat.at[j], m.gp.at[slot], m.r_gp.at[slot], at(d, partner))
     settle(held)
     lax.fori_loop(0, 1, backward, 0)
+    pl.semaphore_wait(m.passed, n_rep - 1)
     for place, (slot, j) in enumerate(held):
-        take(m.gp.at[slot], m.s_gp.at[slot], m.r_gp.at[slot])
+        take(m.gp.at[slot], m.r_gp.at[slot])
         m.sb[slot] = (m.gfeat[j].astype(F32) + m.gp[slot].astype(F32)).astype(BF16)
         if place < 2:
             t = 2 * c + slot - 1
             for q in range(n_rep):
-                push(m.sb.at[slot, q], m.rf.at[t, y], m.s_rf.at[slot - 1, q], m.r_rf.at[t, y],
+                push(m.sb.at[slot, q], m.rf.at[t, y], m.r_rf,
                      at(dom_at((c + 1) * (2 * slot - 3)), q))
     for i, q in enumerate(peers):
-        push(m.sb.at[0, q], m.ro.at[c, y], m.s_ro.at[i], m.r_ro.at[c, y], at(d, q))
-    m.ro[c, y] = m.sb[0, r]
+        push(m.sb.at[0, q], m.ro.at[r], m.r_ro, at(d, q))
+    m.ro[r] = m.sb[0, r]
     lax.fori_loop(1, pairs // BACK_GROUP, backward, 0)
     for t, o in enumerate(OFFSETS):
         m.side[t] = m.far[sum_at(3, own + t)]
-        push(m.side.at[t], m.rs.at[t], m.s_rs.at[t], m.r_rs.at[t], at(dom_at(-o), r))
-    take(m.slope.at[mate], m.s_adj.at[2], m.r_adj.at[2])
-    take(m.packed.at[mate], m.s_adj.at[3], m.r_adj.at[3])
+        push(m.side.at[t], m.rs.at[t], m.r_rs, at(dom_at(-o), r))
+    take(m.state.at[0], m.r_state)
     pick = (lax.broadcasted_iota(jnp.int32, (channels, share), 0)
             == lax.broadcasted_iota(jnp.int32, (channels, share), 1) + r * share).astype(BF16)
-    cols = mm(m.slope[...].reshape(atoms, channels), pick).astype(BF16)
-    m.mix[...] = tn(m.packed[...].reshape(atoms, channels), cols).reshape(m.mix.shape)
+    cols = mm(m.state[0].reshape(atoms, channels), pick).astype(BF16)
+    m.mix[...] = tn(m.state[1].reshape(atoms, channels), cols).reshape(m.mix.shape)
     def mix_copy(i):
         to = lax.rem(d + i, n_dom)
-        return pltpu.make_async_remote_copy(m.mix.at[to], m.rm.at[d], m.s_mix.at[i], m.r_mix.at[d],
+        return pltpu.make_async_remote_copy(m.mix.at[to], m.rm.at[d], m.sent, m.r_mix,
                                             device_id=at(to, r), device_id_type=MESH)
 
     lax.fori_loop(1, n_dom, lambda i, _: (mix_copy(i).start(), 0)[1], 0)
-    for q in peers:
-        take(m.ro.at[lax.rem(q, 2), lax.div(q, 2)], m.s_ro.at[0], m.r_ro.at[lax.rem(q, 2), lax.div(q, 2)])
-    total = jnp.concatenate([m.ro[j, 0].astype(F32) + m.ro[j, 1].astype(F32) for j in range(own)], axis=1)
-    for t in range(4):
-        for q in range(2):
-            take(m.rf.at[t, q], m.s_rf.at[0, 0], m.r_rf.at[t, q])
+    take(m.ro.at[:n_rep - 1], m.r_ro)
+    total = jnp.concatenate([m.ro[j].astype(F32) + m.ro[own + j].astype(F32) for j in range(own)], axis=1)
+    take(m.rf, m.r_rf)
     both = nt(jnp.concatenate([m.rf[t].reshape(2 * share, TILE) for t in range(4)], axis=1), m.hot[...])
     m.part[r] = (total + (both[:share] + both[share:])).astype(BF16)
-    for i, q in enumerate(peers):
-        push(m.part.at[r], m.part.at[r], m.s_part.at[i], m.r_part.at[r], at(d, q))
-    for t in range(4):
-        take(m.rs.at[t], m.s_rs.at[t], m.r_rs.at[t])
+    push(m.part.at[r], m.part.at[r], m.r_part.at[0], at(d, across))
+    push(m.part.at[r], m.part.at[r], m.r_part.at[1], at(d, partner))
+    take(m.rs, m.r_rs)
     left = jnp.concatenate([jnp.concatenate(split3(m.rs[t]), axis=0) for t in range(4)], axis=1)
     spots = nt(left, m.hot[...])
     m.pside[r] = (jnp.concatenate([m.far[sum_at(3, j)] + m.near[j] for j in range(own)], axis=1)
                   + (spots[0:16] + spots[16:32] + spots[32:48]))
     for i, q in enumerate(peers):
-        push(m.pside.at[r], m.pside.at[r], m.s_side.at[i], m.r_side.at[r], at(d, q))
-
-    def mix_add(i, value):
-        frm = lax.rem(d + i, n_dom)
-        take(m.rm.at[frm], m.s_mix.at[0], m.r_mix.at[frm])
-        return value + m.rm[frm]
-
-    m.out_mix[...] = lax.fori_loop(1, n_dom, mix_add, m.mix[d])
-    for q in peers:
-        take(m.pside.at[q], m.s_side.at[0], m.r_side.at[q])
+        push(m.pside.at[r], m.pside.at[r], m.r_side, at(d, q))
+    take(m.part.at[across], m.r_part.at[0])
+    push(m.part.at[across], m.part.at[across], m.r_part.at[2], at(d, partner))
+
+    take(m.rm.at[:n_dom - 1], m.r_mix)
+    m.out_mix[...] = lax.fori_loop(1, n_dom, lambda i, v: v + m.rm[lax.rem(d + i, n_dom)], m.mix[d])
+    take(m.pside.at[:n_rep - 1], m.r_side)
     final = (m.pside[0] + m.pside[1]) + (m.pside[2] + m.pside[3])
     m.out_force[...] = final[0:3]
     m.out_virial[...] = final[8:14]
-    for q in peers:
-        take(m.part.at[q], m.s_part.at[0], m.r_part.at[q])
+    take(m.part.at[partner], m.r_part.at[1])
+    take(m.part.at[partner], m.r_part.at[2])
     m.out_feat[...] = nt(m.eye[:atoms, :atoms], m.part[...].reshape(channels, atoms)).astype(BF16)
     for copy in started:
         copy.wait_send()
@@ -480,25 +470,20 @@
         "near": pltpu.VMEM((own, 16, TILE), F32),
         "msg": pltpu.VMEM((2, TILE // 2, channels), BF16), "msg_in": pltpu.VMEM((2, TILE // 2, channels), BF16),
         "chip": pltpu.VMEM((2, TILE // 2, channels), BF16), "chip_in": pltpu.VMEM((2, TILE // 2, channels), BF16),
-        "adjoint": pltpu.VMEM((own, 2, TILE // 2, channels), BF16), "slope": pltpu.VMEM((own, 2, TILE // 2, channels), BF16),
-        "packed": pltpu.VMEM((own, 2, TILE // 2, channels), BF16),
+        "adjoint": pltpu.VMEM((own, 2, TILE // 2, channels), BF16), "state": pltpu.VMEM((2, own, 2, TILE // 2, channels), BF16),
         "weights": pltpu.VMEM((own * kinds, TILE, channels), BF16),
         "gfeat": pltpu.VMEM((n_ext, *quarters), BF16), "side": pltpu.VMEM((4, 16, TILE), F32),
         "gp": pltpu.VMEM((3, *quarters), BF16),
         "sb": pltpu.VMEM((3, *quarters), BF16),
-        "rf": pltpu.VMEM((4, 2, *quarters[1:]), BF16), "ro": pltpu.VMEM((own, 2, *quarters[1:]), BF16), "rs": pltpu.VMEM((4, 16, TILE), F32),
+        "rf": pltpu.VMEM((4, 2, *quarters[1:]), BF16), "ro": pltpu.VMEM(quarters, BF16), "rs": pltpu.VMEM((4, 16, TILE), F32),
         "mix": pltpu.VMEM((n_dom, mix_rows, mix_cols), F32), "rm": pltpu.VMEM((n_dom, mix_rows, mix_cols), F32),
         "part": pltpu.VMEM((n_rep, channels // n_rep, atoms), BF16),
         "eye": pltpu.VMEM((max(atoms, channels),) * 2, BF16),
         "pside": pltpu.VMEM((n_rep, 16, atoms), F32),
-        "load": dma((len(INPUTS),)), "s_plan": dma, "s_pos": dma((2, 2)), "r_pos": dma((4,)),
-        "s_feat": dma((2,)), "r_feat": dma((4,)), "s_relay": dma((2,)), "r_relay": dma((4,)),
-        "s_msg": dma((2,)), "r_msg": dma((2,)), "s_chip": dma((2,)), "r_chip": dma((2,)), "s_adj": dma((4,)), "r_adj": dma((4,)),
-        "s_gp": dma((3,)), "r_gp": dma((3,)),
-        "s_rf": dma((2, n_rep)), "r_rf": dma((4, 2)),
-        "s_ro": dma((n_rep,)), "r_ro": dma((own, 2)), "s_rs": dma((4,)), "r_rs": dma((4,)),
-        "s_mix": dma((n_dom,)), "r_mix": dma((n_dom,)), "s_part": dma((n_rep,)), "r_part": dma((n_rep,)),
-        "s_side": dma((n_rep,)), "r_side": dma((n_rep,)),
+        "load": dma((3,)), "s_plan": dma, "sent": dma, "passed": pltpu.SemaphoreType.REGULAR, "r_pos": dma,
+        "r_feat": dma((2,)), "r_relay": dma, "r_msg": dma((2,)), "r_chip": dma((2,)), "r_adj": dma,
+        "r_state": dma, "r_gp": dma((3,)), "r_rf": dma, "r_ro": dma, "r_rs": dma, "r_mix": dma,
+        "r_part": dma((3,)), "r_side": dma,
     }
 
     def shape(dims, dtype):

time: 35.5 us -> 34.3 us (0.966)
  Pallas kernels: 34.7 us -> 33.4 us
    pallas_call x1, Pallas kernels: 34 us -> 32.7 us  [on_device(): pl.pallas_call(functools.partial(kernel, INPUTS + OUTPUTS + tuple(scratch...]
where the time goes in v4:
time: 34.3 us; the launch traced here: 34 us
  Pallas kernels  33.4 us (97%)
  between operations  0.64 us (2%)
    pallas_call x1, Pallas kernels, on_device(): pl.pallas_call(functools.partial(kernel, INPUTS + OUTPUTS + tuple(scratch...  32.7 us
    pallas_call x1, Pallas kernels, on_device(): pl.pallas_call(copy_out, out_shape=tuple((shape(a.shape, a.dtype) for a i...  0.7 us

profile of v4, /device:TPU:0, one launch (start us, length us, event | category | flops | bytes accessed | tf_op | source)
XLA Modules:
  0.0 34.0 jit_solution(10222200396305159266)
XLA Ops:
  0.6 32.7 %layer.1 = (bf16[256,256]{1,0:T(8,128)(2,1)S(1)}, f32[3,256]{1,0:T(4,128)S(1)}, f32[6,256]{1,0:T(8,128)S(1)}, f32[32,64]{1,0:T(8,128)S(1)}) custom-call(bf16[256,256]{1,0:T(8,128)(2,1)} %refs_0_.1, f32[3,256]{1,0:T(4,128)} %refs_1_.1, s32[4,128]{1,0:T(4,128)} %refs_2_.1, bf16[8,256,256]{2,1,0:T(8,128)(2,1)} %refs_3_.1, bf16[256,256]{1,0:T(8,128)(2,1)} %refs_4_.1, ...), custom_call_target="tpu_custom_call" | custom-call | tf_op jit(solution)/shard_map/layer/pallas_call | solution.py:492
  33.3 0.7 %copy_out.1 = (bf16[256,256]{1,0:T(8,128)(2,1)}, f32[3,256]{1,0:T(4,128)}, f32[6,256]{1,0:T(8,128)}, f32[32,64]{1,0:T(8,128)}) custom-call(bf16[256,256]{1,0:T(8,128)(2,1)S(1)} %get-tuple-element.8.a, f32[3,256]{1,0:T(4,128)S(1)} %get-tuple-element.9.b, f32[6,256]{1,0:T(8,128)S(1)} %get-tuple-element.10.c, f32[32,64]{1,0:T(8,128)S(1)} %get-tuple-element.11.d), custom_call_target="tpu_custom_call" | custom-call | tf_op jit(solution)/shard_map/copy_out/pallas_call | solution.py:504

commit v5 on v4

--- a/solution.py
+++ b/solution.py
@@ -66,6 +66,7 @@
     mate = 1 - c
     partner = r + 1 - 2 * c
     across = r + 2 - 4 * y
+    cross = across + 1 - 2 * c
     atoms, channels = m.feat.shape
     own = atoms // TILE
     late = lax.div(n_dom - 1 - d, n_dom // 2)
@@ -129,6 +130,15 @@
         m.sendp[q] = jnp.dot(m.pos[...], hot, precision=lax.Precision.HIGHEST, preferred_element_type=F32)
     for q in range(2):
         m.sendf[q] = tn(hots[q], m.feat[...]).astype(BF16)
+    pl.semaphore_wait(barrier, 4 + n_rep - 1 + n_dom - 1)
+    for q in (late, 1 - late):
+        for i, rep in enumerate((r, partner)):
+            push(m.sendp.at[q], m.recvp.at[2 * c + q], m.r_pos,
+                 at(dom_at((c + 1) * (1 - 2 * q)), rep))
+    for q in (late, 1 - late):
+        push(m.sendf.at[q], m.ext.at[own + 2 * c + q], m.r_feat.at[q],
+             at(dom_at((c + 1) * (1 - 2 * q)), r))
+
     for copy in loads[1]:
         copy.wait()
     m.raw[...] = jnp.zeros_like(m.raw)
@@ -169,15 +179,6 @@
         m.tiles[j] = m.pos[:, j * TILE:(j + 1) * TILE]
         m.ext[j] = m.feat[j * TILE:(j + 1) * TILE, :]
         columns(j)
-    pl.semaphore_wait(barrier, 4 + n_rep - 1 + n_dom - 1)
-    for q in (late, 1 - late):
-        for i, rep in enumerate((r, partner)):
-            push(m.sendp.at[q], m.recvp.at[2 * c + q], m.r_pos,
-                 at(dom_at((c + 1) * (1 - 2 * q)), rep))
-    for q in (late, 1 - late):
-        push(m.sendf.at[q], m.ext.at[own + 2 * c + q], m.r_feat.at[q],
-             at(dom_at((c + 1) * (1 - 2 * q)), r))
-
     for q in peers:
         pl.semaphore_signal(m.passed, inc=1, device_id=at(d, q), device_id_type=MESH)
     m.sums[0] = jnp.zeros_like(m.sums[0])
@@ -192,6 +193,8 @@
         table(j)
     for copy in loads[2]:
         copy.wait()
+    for k in range(kinds):
+        m.radmix[k] = mm(m.radial[k], m.mixing[...]).astype(BF16)
     take(m.recvp, m.r_pos)
     for t in range(4):
         m.tiles[own + t] = m.recvp[t]
@@ -261,13 +264,13 @@
     for q in range(2):
         push(m.msg.at[q], m.msg_in.at[q], m.r_msg.at[q], at(d, partner))
     value = message(c).reshape(m.msg.shape)
-    for t in range(4):
-        columns(own + t)
-        table(own + t)
     for q in range(2):
         take(m.msg_in.at[q], m.r_msg.at[q])
         m.chip[q] = (value[q] + m.msg_in[q].astype(F32)).astype(BF16)
         push(m.chip.at[q], m.chip_in.at[q], m.r_chip.at[q], at(d, across))
+    for t in range(4):
+        columns(own + t)
+        table(own + t)
     lax.fori_loop(0, pairs // GROUP, transposed, 0)
     for q in range(2):
         take(m.chip_in.at[q], m.r_chip.at[q])
@@ -275,17 +278,15 @@
         mixed = mm(low, m.mixing[...])
         sig = jax.nn.sigmoid(mixed)
         slope = (m.readout[...] * sig * (1.0 + mixed * (1.0 - sig))).astype(BF16)
-        m.adjoint[c, q] = nt(slope, m.mixing[...]).astype(BF16)
-        push(m.adjoint.at[c, q], m.adjoint.at[c, q], m.r_adj, at(d, partner))
-        m.state[0, c, q] = slope
-        m.state[1, c, q] = low
-    push(m.state.at[0, c], m.state.at[0, c], m.r_state, at(d, partner))
-    push(m.state.at[1, c], m.state.at[1, c], m.r_state, at(d, partner))
-
-    take(m.adjoint.at[mate], m.r_adj)
-    adjoint = m.adjoint[...].reshape(atoms, channels)
+        m.slope[c, q] = slope
+        push(m.slope.at[c, q], m.slope.at[c, q], m.r_slope, at(d, partner))
+        m.packed[c, q] = low
+    push(m.packed.at[c], m.packed.at[c], m.r_packed, at(d, partner))
+
+    take(m.slope.at[mate], m.r_slope)
+    slope = m.slope[...].reshape(atoms, channels)
     for k in range(kinds):
-        wide = nt(adjoint, m.radial[k]).astype(BF16)
+        wide = nt(slope, m.radmix[k]).astype(BF16)
         for j in range(own):
             m.weights[j * kinds + k] = wide[j * TILE:(j + 1) * TILE]
 
@@ -373,21 +374,21 @@
         m.sb[slot] = (m.gfeat[j].astype(F32) + m.gp[slot].astype(F32)).astype(BF16)
         if place < 2:
             t = 2 * c + slot - 1
-            for q in range(n_rep):
+            for q in (across, cross, r, partner):
                 push(m.sb.at[slot, q], m.rf.at[t, y], m.r_rf,
                      at(dom_at((c + 1) * (2 * slot - 3)), q))
-    for i, q in enumerate(peers):
+    for q in (across, cross, partner):
         push(m.sb.at[0, q], m.ro.at[r], m.r_ro, at(d, q))
     m.ro[r] = m.sb[0, r]
     lax.fori_loop(1, pairs // BACK_GROUP, backward, 0)
     for t, o in enumerate(OFFSETS):
-        m.side[t] = m.far[sum_at(3, own + t)]
+        m.side[t] = m.far[sum_at(3, own + t)].astype(BF16)
         push(m.side.at[t], m.rs.at[t], m.r_rs, at(dom_at(-o), r))
-    take(m.state.at[0], m.r_state)
+    take(m.packed.at[mate], m.r_packed)
     pick = (lax.broadcasted_iota(jnp.int32, (channels, share), 0)
             == lax.broadcasted_iota(jnp.int32, (channels, share), 1) + r * share).astype(BF16)
-    cols = mm(m.state[0].reshape(atoms, channels), pick).astype(BF16)
-    m.mix[...] = tn(m.state[1].reshape(atoms, channels), cols).reshape(m.mix.shape)
+    cols = mm(m.slope[...].reshape(atoms, channels), pick).astype(BF16)
+    m.mix[...] = tn(m.packed[...].reshape(atoms, channels), cols).reshape(m.mix.shape)
     def mix_copy(i):
         to = lax.rem(d + i, n_dom)
         return pltpu.make_async_remote_copy(m.mix.at[to], m.rm.at[d], m.sent, m.r_mix,
@@ -399,26 +400,21 @@
     take(m.rf, m.r_rf)
     both = nt(jnp.concatenate([m.rf[t].reshape(2 * share, TILE) for t in range(4)], axis=1), m.hot[...])
     m.part[r] = (total + (both[:share] + both[share:])).astype(BF16)
-    push(m.part.at[r], m.part.at[r], m.r_part.at[0], at(d, across))
-    push(m.part.at[r], m.part.at[r], m.r_part.at[1], at(d, partner))
+    for q in (across, cross, partner):
+        push(m.part.at[r], m.part.at[r], m.r_part, at(d, q))
     take(m.rs, m.r_rs)
-    left = jnp.concatenate([jnp.concatenate(split3(m.rs[t]), axis=0) for t in range(4)], axis=1)
-    spots = nt(left, m.hot[...])
-    m.pside[r] = (jnp.concatenate([m.far[sum_at(3, j)] + m.near[j] for j in range(own)], axis=1)
-                  + (spots[0:16] + spots[16:32] + spots[32:48]))
-    for i, q in enumerate(peers):
+    spots = nt(jnp.concatenate([m.rs[t] for t in range(4)], axis=1), m.hot[...])
+    here = jnp.concatenate([m.far[sum_at(3, j)] + m.near[j] for j in range(own)], axis=1)
+    m.pside[r] = (here + spots).astype(BF16)
+    for q in (across, cross, partner):
         push(m.pside.at[r], m.pside.at[r], m.r_side, at(d, q))
-    take(m.part.at[across], m.r_part.at[0])
-    push(m.part.at[across], m.part.at[across], m.r_part.at[2], at(d, partner))
-
     take(m.rm.at[:n_dom - 1], m.r_mix)
     m.out_mix[...] = lax.fori_loop(1, n_dom, lambda i, v: v + m.rm[lax.rem(d + i, n_dom)], m.mix[d])
     take(m.pside.at[:n_rep - 1], m.r_side)
-    final = (m.pside[0] + m.pside[1]) + (m.pside[2] + m.pside[3])
+    final = sum(m.pside[q].astype(F32) for q in range(n_rep))
     m.out_force[...] = final[0:3]
     m.out_virial[...] = final[8:14]
-    take(m.part.at[partner], m.r_part.at[1])
-    take(m.part.at[partner], m.r_part.at[2])
+    take(m.part.at[:n_rep - 1], m.r_part)
     m.out_feat[...] = nt(m.eye[:atoms, :atoms], m.part[...].reshape(channels, atoms)).astype(BF16)
     for copy in started:
         copy.wait_send()
@@ -426,8 +422,8 @@
 
 
 def copy_out(a, b, c, d, a_h, b_h, c_h, d_h, sem):
-    copies = [pltpu.make_async_copy(src, dst, sem.at[i])
-              for i, (src, dst) in enumerate(((a, a_h), (b, b_h), (c, c_h), (d, d_h)))]
+    copies = [pltpu.make_async_copy(src, dst, sem)
+              for src, dst in ((a, a_h), (b, b_h), (c, c_h), (d, d_h))]
     for copy in copies:
         copy.start()
     for copy in copies:
@@ -470,20 +466,21 @@
         "near": pltpu.VMEM((own, 16, TILE), F32),
         "msg": pltpu.VMEM((2, TILE // 2, channels), BF16), "msg_in": pltpu.VMEM((2, TILE // 2, channels), BF16),
         "chip": pltpu.VMEM((2, TILE // 2, channels), BF16), "chip_in": pltpu.VMEM((2, TILE // 2, channels), BF16),
-        "adjoint": pltpu.VMEM((own, 2, TILE // 2, channels), BF16), "state": pltpu.VMEM((2, own, 2, TILE // 2, channels), BF16),
+        "slope": pltpu.VMEM((own, 2, TILE // 2, channels), BF16),
+        "packed": pltpu.VMEM((own, 2, TILE // 2, channels), BF16), "radmix": pltpu.VMEM(radial.shape, BF16),
         "weights": pltpu.VMEM((own * kinds, TILE, channels), BF16),
-        "gfeat": pltpu.VMEM((n_ext, *quarters), BF16), "side": pltpu.VMEM((4, 16, TILE), F32),
+        "gfeat": pltpu.VMEM((n_ext, *quarters), BF16), "side": pltpu.VMEM((4, 16, TILE), BF16),
         "gp": pltpu.VMEM((3, *quarters), BF16),
         "sb": pltpu.VMEM((3, *quarters), BF16),
-        "rf": pltpu.VMEM((4, 2, *quarters[1:]), BF16), "ro": pltpu.VMEM(quarters, BF16), "rs": pltpu.VMEM((4, 16, TILE), F32),
+        "rf": pltpu.VMEM((4, 2, *quarters[1:]), BF16), "ro": pltpu.VMEM(quarters, BF16), "rs": pltpu.VMEM((4, 16, TILE), BF16),
         "mix": pltpu.VMEM((n_dom, mix_rows, mix_cols), F32), "rm": pltpu.VMEM((n_dom, mix_rows, mix_cols), F32),
         "part": pltpu.VMEM((n_rep, channels // n_rep, atoms), BF16),
         "eye": pltpu.VMEM((max(atoms, channels),) * 2, BF16),
-        "pside": pltpu.VMEM((n_rep, 16, atoms), F32),
+        "pside": pltpu.VMEM((n_rep, 16, atoms), BF16),
         "load": dma((3,)), "s_plan": dma, "sent": dma, "passed": pltpu.SemaphoreType.REGULAR, "r_pos": dma,
-        "r_feat": dma((2,)), "r_relay": dma, "r_msg": dma((2,)), "r_chip": dma((2,)), "r_adj": dma,
-        "r_state": dma, "r_gp": dma((3,)), "r_rf": dma, "r_ro": dma, "r_rs": dma, "r_mix": dma,
-        "r_part": dma((3,)), "r_side": dma,
+        "r_feat": dma((2,)), "r_relay": dma, "r_msg": dma((2,)), "r_chip": dma((2,)), "r_slope": dma,
+        "r_packed": dma, "r_gp": dma((3,)), "r_rf": dma, "r_ro": dma, "r_rs": dma, "r_mix": dma,
+        "r_part": dma, "r_side": dma,
     }
 
     def shape(dims, dtype):
@@ -506,7 +503,7 @@
         out_shape=tuple(shape(a.shape, a.dtype) for a in results),
         in_specs=[VMEM] * 4,
         out_specs=(HBM,) * 4,
-        scratch_shapes=[dma((4,))],
+        scratch_shapes=[dma],
         compiler_params=pltpu.CompilerParams(vmem_limit_bytes=4 << 20),
         name="copy_out",
     )(*results)

time: 34.3 us -> 33.4 us (0.974)
  Pallas kernels: 33.4 us -> 32.6 us
    pallas_call x1, Pallas kernels: 32.7 us -> 32 us  [on_device(): pl.pallas_call(functools.partial(kernel, INPUTS + OUTPUTS + tuple(scratch...]
where the time goes in v5:
time: 33.4 us; the launch traced here: 33.3 us
  Pallas kernels  32.6 us (98%)
  between operations  0.64 us (2%)
    pallas_call x1, Pallas kernels, on_device(): pl.pallas_call(functools.partial(kernel, INPUTS + OUTPUTS + tuple(scratch...  32 us

profile of v5, /device:TPU:0, one launch (start us, length us, event | category | flops | bytes accessed | tf_op | source)
XLA Modules:
  0.0 33.3 jit_solution(14652694231936883049)
XLA Ops:
  0.6 32.0 %layer.1 = (bf16[256,256]{1,0:T(8,128)(2,1)S(1)}, f32[3,256]{1,0:T(4,128)S(1)}, f32[6,256]{1,0:T(8,128)S(1)}, f32[32,64]{1,0:T(8,128)S(1)}) custom-call(bf16[256,256]{1,0:T(8,128)(2,1)} %refs_0_.1, f32[3,256]{1,0:T(4,128)} %refs_1_.1, s32[4,128]{1,0:T(4,128)} %refs_2_.1, bf16[8,256,256]{2,1,0:T(8,128)(2,1)} %refs_3_.1, bf16[256,256]{1,0:T(8,128)(2,1)} %refs_4_.1, ...), custom_call_target="tpu_custom_call" | custom-call | tf_op jit(solution)/shard_map/layer/pallas_call | solution.py:489
  32.6 0.7 %copy_out.1 = (bf16[256,256]{1,0:T(8,128)(2,1)}, f32[3,256]{1,0:T(4,128)}, f32[6,256]{1,0:T(8,128)}, f32[32,64]{1,0:T(8,128)}) custom-call(bf16[256,256]{1,0:T(8,128)(2,1)S(1)} %get-tuple-element.8.a, f32[3,256]{1,0:T(4,128)S(1)} %get-tuple-element.9.b, f32[6,256]{1,0:T(8,128)S(1)} %get-tuple-element.10.c, f32[32,64]{1,0:T(8,128)S(1)} %get-tuple-element.11.d), custom_call_target="tpu_custom_call" | custom-call | tf_op jit(solution)/shard_map/copy_out/pallas_call | solution.py:501

commit v6 on v5

--- a/solution.py
+++ b/solution.py
@@ -12,7 +12,7 @@
 OFFSETS = (1, -1, 2, -2)
 CELL = 2.0
 GROUP = 4
-WIDE_GROUP = 24
+WIDE_GROUP = 48
 BACK_GROUP = 12
 LOG2E = 1.4426950408889634
 F32 = jnp.float32
@@ -73,6 +73,8 @@
     pairs = m.home.shape[0]
     kinds = m.radial.shape[0]
     n_ext = m.tiles.shape[0]
+    size = TILE // 2
+    halves = [pl.ds(i * size, size) for i in range(2)]
 
     def dom_at(o):
         return lax.rem(d + o + n_dom, n_dom)
@@ -136,8 +138,9 @@
             push(m.sendp.at[q], m.recvp.at[2 * c + q], m.r_pos,
                  at(dom_at((c + 1) * (1 - 2 * q)), rep))
     for q in (late, 1 - late):
-        push(m.sendf.at[q], m.ext.at[own + 2 * c + q], m.r_feat.at[q],
-             at(dom_at((c + 1) * (1 - 2 * q)), r))
+        for rows in halves:
+            push(m.sendf.at[q, rows], m.ext.at[own + 2 * c + q, rows], m.r_feat.at[q, rows.start // size],
+                 at(dom_at((c + 1) * (1 - 2 * q)), r))
 
     for copy in loads[1]:
         copy.wait()
@@ -184,7 +187,7 @@
     m.sums[0] = jnp.zeros_like(m.sums[0])
     m.carry[...] = jnp.zeros_like(m.carry)
     for t in range(4):
-        m.hot[:, t * TILE:(t + 1) * TILE] = (iota == m.rows[t:t + 1, :]).astype(F32).astype(BF16)
+        m.hot[t % 2, :, t // 2 * TILE:(t // 2 + 1) * TILE] = (iota == m.rows[t:t + 1, :]).astype(F32).astype(BF16)
     m.far[0] = jnp.zeros_like(m.far[0])
     m.near[...] = jnp.zeros_like(m.near)
     m.eye[...] = (lax.broadcasted_iota(jnp.int32, m.eye.shape, 0)
@@ -225,10 +228,11 @@
 
     half_steps = pairs // GROUP // 2
     lax.fori_loop(0, half_steps, kernels, 0)
-    for q in range(2):
-        t = 2 * c + q
-        take(m.ext.at[own + t], m.r_feat.at[q])
-        push(m.ext.at[own + t], m.ext.at[own + t], m.r_relay, at(d, partner))
+    for q in (late, 1 - late):
+        t = own + 2 * c + q
+        for rows in halves:
+            take(m.ext.at[t, rows], m.r_feat.at[q, rows.start // size])
+            push(m.ext.at[t, rows], m.ext.at[t, rows], m.r_relay, at(d, partner))
     lax.fori_loop(half_steps, pairs // GROUP, kernels, 0)
     plan_copy.wait()
     take(m.ext.at[pl.ds(own + 2 * mate, 2)], m.r_relay)
@@ -367,20 +371,19 @@
     for slot, j in away:
         push(m.gfeat.at[j], m.gp.at[slot], m.r_gp.at[slot], at(d, partner))
     settle(held)
-    lax.fori_loop(0, 1, backward, 0)
+    lax.fori_loop(0, 2 - c, backward, 0)
     pl.semaphore_wait(m.passed, n_rep - 1)
     for place, (slot, j) in enumerate(held):
         take(m.gp.at[slot], m.r_gp.at[slot])
         m.sb[slot] = (m.gfeat[j].astype(F32) + m.gp[slot].astype(F32)).astype(BF16)
         if place < 2:
-            t = 2 * c + slot - 1
             for q in (across, cross, r, partner):
-                push(m.sb.at[slot, q], m.rf.at[t, y], m.r_rf,
+                push(m.sb.at[slot, q], m.rf.at[slot - 1, c, y], m.r_rf.at[slot - 1],
                      at(dom_at((c + 1) * (2 * slot - 3)), q))
     for q in (across, cross, partner):
         push(m.sb.at[0, q], m.ro.at[r], m.r_ro, at(d, q))
     m.ro[r] = m.sb[0, r]
-    lax.fori_loop(1, pairs // BACK_GROUP, backward, 0)
+    lax.fori_loop(2 - c, pairs // BACK_GROUP, backward, 0)
     for t, o in enumerate(OFFSETS):
         m.side[t] = m.far[sum_at(3, own + t)].astype(BF16)
         push(m.side.at[t], m.rs.at[t], m.r_rs, at(dom_at(-o), r))
@@ -397,25 +400,42 @@
     lax.fori_loop(1, n_dom, lambda i, _: (mix_copy(i).start(), 0)[1], 0)
     take(m.ro.at[:n_rep - 1], m.r_ro)
     total = jnp.concatenate([m.ro[j].astype(F32) + m.ro[own + j].astype(F32) for j in range(own)], axis=1)
-    take(m.rf, m.r_rf)
-    both = nt(jnp.concatenate([m.rf[t].reshape(2 * share, TILE) for t in range(4)], axis=1), m.hot[...])
-    m.part[r] = (total + (both[:share] + both[share:])).astype(BF16)
-    for q in (across, cross, partner):
-        push(m.part.at[r], m.part.at[r], m.r_part, at(d, q))
+    def gather(group):
+        take(m.rf.at[group], m.r_rf.at[group])
+        both = nt(jnp.concatenate([m.rf[group, i].reshape(2 * share, TILE) for i in range(2)], axis=1), m.hot[group])
+        return both[:share] + both[share:]
+
+    total = total + gather(1 - late)
+    m.part[r] = (total + gather(late)).astype(BF16)
+    low, high = [pl.ds(i * share // 2, share // 2) for i in range(2)]
+    push(m.part.at[r, high], m.part.at[r, high], m.r_part.at[0], at(d, across))
+    push(m.part.at[r, low], m.part.at[r, low], m.r_part.at[1], at(d, across))
+    push(m.part.at[r, low], m.part.at[r, low], m.r_part.at[1], at(d, cross))
+    push(m.part.at[r], m.part.at[r], m.r_part.at[2], at(d, partner))
     take(m.rs, m.r_rs)
-    spots = nt(jnp.concatenate([m.rs[t] for t in range(4)], axis=1), m.hot[...])
+    spots = sum(nt(jnp.concatenate([m.rs[i], m.rs[i + 2]], axis=1), m.hot[i]) for i in range(2))
     here = jnp.concatenate([m.far[sum_at(3, j)] + m.near[j] for j in range(own)], axis=1)
     m.pside[r] = (here + spots).astype(BF16)
     for q in (across, cross, partner):
         push(m.pside.at[r], m.pside.at[r], m.r_side, at(d, q))
+    def finish(half):
+        width = channels // 2
+        turned = nt(m.eye[:atoms, :atoms], m.part[pl.ds(2 * half, 2)].reshape(width, atoms))
+        m.out_feat[:, pl.ds(pl.multiple_of(half * width, TILE), width)] = turned.astype(BF16)
+
+    take(m.part.at[partner], m.r_part.at[2])
+    finish(y)
+    take(m.part.at[across, high], m.r_part.at[0])
+    push(m.part.at[across, high], m.part.at[across, high], m.r_part.at[3], at(d, partner))
     take(m.rm.at[:n_dom - 1], m.r_mix)
     m.out_mix[...] = lax.fori_loop(1, n_dom, lambda i, v: v + m.rm[lax.rem(d + i, n_dom)], m.mix[d])
     take(m.pside.at[:n_rep - 1], m.r_side)
     final = sum(m.pside[q].astype(F32) for q in range(n_rep))
     m.out_force[...] = final[0:3]
     m.out_virial[...] = final[8:14]
-    take(m.part.at[:n_rep - 1], m.r_part)
-    m.out_feat[...] = nt(m.eye[:atoms, :atoms], m.part[...].reshape(channels, atoms)).astype(BF16)
+    take(m.part.at[across], m.r_part.at[1])
+    take(m.part.at[cross, high], m.r_part.at[3])
+    finish(1 - y)
     for copy in started:
         copy.wait_send()
     lax.fori_loop(1, n_dom, lambda i, _: (mix_copy(i).wait_send(), 0)[1], 0)
@@ -458,7 +478,7 @@
         "recvp": pltpu.VMEM((4, 3, TILE), F32), "ext": pltpu.VMEM((n_ext, TILE, channels), BF16),
         "tiles": pltpu.VMEM((n_ext, 3, TILE), F32), "col": pltpu.VMEM((n_ext, 3, TILE, TILE), F32),
         "moments": pltpu.VMEM((n_ext, 80, TILE), BF16),
-        "sided": pltpu.VMEM((own, 2, 80, 2 * TILE), BF16), "hot": pltpu.VMEM((atoms, 4 * TILE), BF16),
+        "sided": pltpu.VMEM((own, 2, 80, 2 * TILE), BF16), "hot": pltpu.VMEM((2, atoms, 2 * TILE), BF16),
         "first": pltpu.VMEM((n_ext, 8, TILE), F32), "second": pltpu.VMEM((n_ext, 8, TILE), F32),
         "kern_ab": pltpu.VMEM((pairs, TILE, TILE), BF16), "kern_ba": pltpu.VMEM((pairs, TILE, TILE), F32),
         "sums": pltpu.VMEM((pairs + 1, TILE, channels), BF16),
@@ -472,15 +492,15 @@
         "gfeat": pltpu.VMEM((n_ext, *quarters), BF16), "side": pltpu.VMEM((4, 16, TILE), BF16),
         "gp": pltpu.VMEM((3, *quarters), BF16),
         "sb": pltpu.VMEM((3, *quarters), BF16),
-        "rf": pltpu.VMEM((4, 2, *quarters[1:]), BF16), "ro": pltpu.VMEM(quarters, BF16), "rs": pltpu.VMEM((4, 16, TILE), BF16),
+        "rf": pltpu.VMEM((2, 2, 2, *quarters[1:]), BF16), "ro": pltpu.VMEM(quarters, BF16), "rs": pltpu.VMEM((4, 16, TILE), BF16),
         "mix": pltpu.VMEM((n_dom, mix_rows, mix_cols), F32), "rm": pltpu.VMEM((n_dom, mix_rows, mix_cols), F32),
         "part": pltpu.VMEM((n_rep, channels // n_rep, atoms), BF16),
         "eye": pltpu.VMEM((max(atoms, channels),) * 2, BF16),
         "pside": pltpu.VMEM((n_rep, 16, atoms), BF16),
         "load": dma((3,)), "s_plan": dma, "sent": dma, "passed": pltpu.SemaphoreType.REGULAR, "r_pos": dma,
-        "r_feat": dma((2,)), "r_relay": dma, "r_msg": dma((2,)), "r_chip": dma((2,)), "r_slope": dma,
-        "r_packed": dma, "r_gp": dma((3,)), "r_rf": dma, "r_ro": dma, "r_rs": dma, "r_mix": dma,
-        "r_part": dma, "r_side": dma,
+        "r_feat": dma((2, 2)), "r_relay": dma, "r_msg": dma((2,)), "r_chip": dma((2,)), "r_slope": dma,
+        "r_packed": dma, "r_gp": dma((3,)), "r_rf": dma((2,)), "r_ro": dma, "r_rs": dma, "r_mix": dma,
+        "r_part": dma((4,)), "r_side": dma,
     }
 
     def shape(dims, dtype):

time: 33.4 us -> 32.9 us (0.985)
  Pallas kernels: 32.6 us -> 32 us
    pallas_call x1, Pallas kernels: 32 us -> 31.4 us  [on_device(): pl.pallas_call(functools.partial(kernel, INPUTS + OUTPUTS + tuple(scratch...]
where the time goes in v6:
time: 32.9 us; the launch traced here: 32.7 us
  Pallas kernels  32 us (97%)
  between operations  0.64 us (2%)
    pallas_call x1, Pallas kernels, on_device(): pl.pallas_call(functools.partial(kernel, INPUTS + OUTPUTS + tuple(scratch...  31.4 us
    pallas_call x1, Pallas kernels, on_device(): pl.pallas_call(copy_out, out_shape=tuple((shape(a.shape, a.dtype) for a i...  0.67 us

profile of v6, /device:TPU:0, one launch (start us, length us, event | category | flops | bytes accessed | tf_op | source)
XLA Modules:
  0.0 32.7 jit_solution(8538405405048440505)
XLA Ops:
  0.6 31.4 %layer.1 = (bf16[256,256]{1,0:T(8,128)(2,1)S(1)}, f32[3,256]{1,0:T(4,128)S(1)}, f32[6,256]{1,0:T(8,128)S(1)}, f32[32,64]{1,0:T(8,128)S(1)}) custom-call(bf16[256,256]{1,0:T(8,128)(2,1)} %refs_0_.1, f32[3,256]{1,0:T(4,128)} %refs_1_.1, s32[4,128]{1,0:T(4,128)} %refs_2_.1, bf16[8,256,256]{2,1,0:T(8,128)(2,1)} %refs_3_.1, bf16[256,256]{1,0:T(8,128)(2,1)} %refs_4_.1, ...), custom_call_target="tpu_custom_call" | custom-call | tf_op jit(solution)/shard_map/layer/pallas_call | solution.py:509
  32.0 0.7 %copy_out.1 = (bf16[256,256]{1,0:T(8,128)(2,1)}, f32[3,256]{1,0:T(4,128)}, f32[6,256]{1,0:T(8,128)}, f32[32,64]{1,0:T(8,128)}) custom-call(bf16[256,256]{1,0:T(8,128)(2,1)S(1)} %get-tuple-element.8.a, f32[3,256]{1,0:T(4,128)S(1)} %get-tuple-element.9.b, f32[6,256]{1,0:T(8,128)S(1)} %get-tuple-element.10.c, f32[32,64]{1,0:T(8,128)S(1)} %get-tuple-element.11.d), custom_call_target="tpu_custom_call" | custom-call | tf_op jit(solution)/shard_map/copy_out/pallas_call | solution.py:521

commit v7 on v6

--- a/solution.py
+++ b/solution.py
@@ -155,7 +155,7 @@
     order_b, end_b = order_pairs(jnp.where(real, raw[2:3], TILE), lanes, subs)
     m.plan_v[...] = jnp.concatenate(
         [order_f, order_b, end_f, end_b, jnp.zeros((4, TILE), jnp.int32)], axis=0)
-    plan_copy = pltpu.make_async_copy(m.plan_v, m.plan, m.s_plan)
+    plan_copy = pltpu.make_async_copy(m.plan_v, m.plan, m.load.at[0])
     plan_copy.start()
 
     def columns(j):
@@ -232,10 +232,10 @@
         t = own + 2 * c + q
         for rows in halves:
             take(m.ext.at[t, rows], m.r_feat.at[q, rows.start // size])
-            push(m.ext.at[t, rows], m.ext.at[t, rows], m.r_relay, at(d, partner))
+            push(m.ext.at[t, rows], m.ext.at[t, rows], m.near_sem.at[2], at(d, partner))
     lax.fori_loop(half_steps, pairs // GROUP, kernels, 0)
     plan_copy.wait()
-    take(m.ext.at[pl.ds(own + 2 * mate, 2)], m.r_relay)
+    take(m.ext.at[pl.ds(own + 2 * mate, 2)], m.near_sem.at[2])
 
     def pair_at(row, i):
         return jnp.clip(m.plan[row, i], 0, pairs - 1)
@@ -266,10 +266,10 @@
 
     m.msg[...] = message(mate).astype(BF16).reshape(m.msg.shape)
     for q in range(2):
-        push(m.msg.at[q], m.msg_in.at[q], m.r_msg.at[q], at(d, partner))
+        push(m.msg.at[q], m.msg_in.at[q], m.near_sem.at[q], at(d, partner))
     value = message(c).reshape(m.msg.shape)
     for q in range(2):
-        take(m.msg_in.at[q], m.r_msg.at[q])
+        take(m.msg_in.at[q], m.near_sem.at[q])
         m.chip[q] = (value[q] + m.msg_in[q].astype(F32)).astype(BF16)
         push(m.chip.at[q], m.chip_in.at[q], m.r_chip.at[q], at(d, across))
     for t in range(4):
@@ -283,11 +283,11 @@
         sig = jax.nn.sigmoid(mixed)
         slope = (m.readout[...] * sig * (1.0 + mixed * (1.0 - sig))).astype(BF16)
         m.slope[c, q] = slope
-        push(m.slope.at[c, q], m.slope.at[c, q], m.r_slope, at(d, partner))
+        push(m.slope.at[c, q], m.slope.at[c, q], m.near_sem.at[3], at(d, partner))
         m.packed[c, q] = low
-    push(m.packed.at[c], m.packed.at[c], m.r_packed, at(d, partner))
-
-    take(m.slope.at[mate], m.r_slope)
+    push(m.packed.at[c], m.packed.at[c], m.near_sem.at[4], at(d, partner))
+
+    take(m.slope.at[mate], m.near_sem.at[3])
     slope = m.slope[...].reshape(atoms, channels)
     for k in range(kinds):
         wide = nt(slope, m.radmix[k]).astype(BF16)
@@ -367,14 +367,15 @@
         for i, (_, j) in enumerate(group):
             m.gfeat[j] = turned[:, i * TILE:(i + 1) * TILE].reshape(n_rep, share, TILE)
 
-    settle(away)
-    for slot, j in away:
-        push(m.gfeat.at[j], m.gp.at[slot], m.r_gp.at[slot], at(d, partner))
+    for group in (away[:1], away[1:]):
+        settle(group)
+        for slot, j in group:
+            push(m.gfeat.at[j], m.gp.at[slot], m.near_sem.at[slot], at(d, partner))
     settle(held)
-    lax.fori_loop(0, 2 - c, backward, 0)
+    lax.fori_loop(0, 2 - 2 * c, backward, 0)
     pl.semaphore_wait(m.passed, n_rep - 1)
     for place, (slot, j) in enumerate(held):
-        take(m.gp.at[slot], m.r_gp.at[slot])
+        take(m.gp.at[slot], m.near_sem.at[slot])
         m.sb[slot] = (m.gfeat[j].astype(F32) + m.gp[slot].astype(F32)).astype(BF16)
         if place < 2:
             for q in (across, cross, r, partner):
@@ -383,11 +384,11 @@
     for q in (across, cross, partner):
         push(m.sb.at[0, q], m.ro.at[r], m.r_ro, at(d, q))
     m.ro[r] = m.sb[0, r]
-    lax.fori_loop(2 - c, pairs // BACK_GROUP, backward, 0)
+    lax.fori_loop(2 - 2 * c, pairs // BACK_GROUP, backward, 0)
     for t, o in enumerate(OFFSETS):
         m.side[t] = m.far[sum_at(3, own + t)].astype(BF16)
         push(m.side.at[t], m.rs.at[t], m.r_rs, at(dom_at(-o), r))
-    take(m.packed.at[mate], m.r_packed)
+    take(m.packed.at[mate], m.near_sem.at[4])
     pick = (lax.broadcasted_iota(jnp.int32, (channels, share), 0)
             == lax.broadcasted_iota(jnp.int32, (channels, share), 1) + r * share).astype(BF16)
     cols = mm(m.slope[...].reshape(atoms, channels), pick).astype(BF16)
@@ -407,34 +408,34 @@
 
     total = total + gather(1 - late)
     m.part[r] = (total + gather(late)).astype(BF16)
-    low, high = [pl.ds(i * share // 2, share // 2) for i in range(2)]
-    push(m.part.at[r, high], m.part.at[r, high], m.r_part.at[0], at(d, across))
-    push(m.part.at[r, low], m.part.at[r, low], m.r_part.at[1], at(d, across))
-    push(m.part.at[r, low], m.part.at[r, low], m.r_part.at[1], at(d, cross))
-    push(m.part.at[r], m.part.at[r], m.r_part.at[2], at(d, partner))
+    low, high = pl.ds(0, share - share // 4), pl.ds(share - share // 4, share // 4)
+    push(m.part.at[r, high], m.part.at[r, high], m.r_chip.at[0], at(d, across))
+    push(m.part.at[r, low], m.part.at[r, low], m.r_chip.at[1], at(d, across))
+    push(m.part.at[r, low], m.part.at[r, low], m.r_chip.at[1], at(d, cross))
+    push(m.part.at[r], m.part.at[r], m.near_sem.at[3], at(d, partner))
     take(m.rs, m.r_rs)
     spots = sum(nt(jnp.concatenate([m.rs[i], m.rs[i + 2]], axis=1), m.hot[i]) for i in range(2))
     here = jnp.concatenate([m.far[sum_at(3, j)] + m.near[j] for j in range(own)], axis=1)
     m.pside[r] = (here + spots).astype(BF16)
     for q in (across, cross, partner):
-        push(m.pside.at[r], m.pside.at[r], m.r_side, at(d, q))
+        push(m.pside.at[r], m.pside.at[r], m.r_pos, at(d, q))
     def finish(half):
         width = channels // 2
         turned = nt(m.eye[:atoms, :atoms], m.part[pl.ds(2 * half, 2)].reshape(width, atoms))
         m.out_feat[:, pl.ds(pl.multiple_of(half * width, TILE), width)] = turned.astype(BF16)
 
-    take(m.part.at[partner], m.r_part.at[2])
+    take(m.part.at[partner], m.near_sem.at[3])
     finish(y)
-    take(m.part.at[across, high], m.r_part.at[0])
-    push(m.part.at[across, high], m.part.at[across, high], m.r_part.at[3], at(d, partner))
+    take(m.part.at[across, high], m.r_chip.at[0])
+    push(m.part.at[across, high], m.part.at[across, high], m.near_sem.at[4], at(d, partner))
     take(m.rm.at[:n_dom - 1], m.r_mix)
     m.out_mix[...] = lax.fori_loop(1, n_dom, lambda i, v: v + m.rm[lax.rem(d + i, n_dom)], m.mix[d])
-    take(m.pside.at[:n_rep - 1], m.r_side)
+    take(m.pside.at[:n_rep - 1], m.r_pos)
     final = sum(m.pside[q].astype(F32) for q in range(n_rep))
     m.out_force[...] = final[0:3]
     m.out_virial[...] = final[8:14]
-    take(m.part.at[across], m.r_part.at[1])
-    take(m.part.at[cross, high], m.r_part.at[3])
+    take(m.part.at[pl.ds(2 * (1 - y), 2), low], m.r_chip.at[1])
+    take(m.part.at[cross, high], m.near_sem.at[4])
     finish(1 - y)
     for copy in started:
         copy.wait_send()
@@ -497,10 +498,9 @@
         "part": pltpu.VMEM((n_rep, channels // n_rep, atoms), BF16),
         "eye": pltpu.VMEM((max(atoms, channels),) * 2, BF16),
         "pside": pltpu.VMEM((n_rep, 16, atoms), BF16),
-        "load": dma((3,)), "s_plan": dma, "sent": dma, "passed": pltpu.SemaphoreType.REGULAR, "r_pos": dma,
-        "r_feat": dma((2, 2)), "r_relay": dma, "r_msg": dma((2,)), "r_chip": dma((2,)), "r_slope": dma,
-        "r_packed": dma, "r_gp": dma((3,)), "r_rf": dma((2,)), "r_ro": dma, "r_rs": dma, "r_mix": dma,
-        "r_part": dma((4,)), "r_side": dma,
+        "load": dma((3,)), "sent": dma, "passed": pltpu.SemaphoreType.REGULAR, "r_pos": dma,
+        "r_feat": dma((2, 2)), "near_sem": dma((5,)), "r_chip": dma((2,)),
+        "r_rf": dma((2,)), "r_ro": dma, "r_rs": dma, "r_mix": dma,
     }
 
     def shape(dims, dtype):

time: 32.9 us -> 32.7 us (level)
  no operation moved by 1% of the time
where the time goes in v7:
time: 32.7 us; the launch traced here: 32.5 us
  Pallas kernels  31.9 us (98%)
  between operations  0.64 us (2%)
    pallas_call x1, Pallas kernels, on_device(): pl.pallas_call(functools.partial(kernel, INPUTS + OUTPUTS + tuple(scratch...  31.2 us
    pallas_call x1, Pallas kernels, on_device(): pl.pallas_call(copy_out, out_shape=tuple((shape(a.shape, a.dtype) for a i...  0.67 us

profile of v7, /device:TPU:0, one launch (start us, length us, event | category | flops | bytes accessed | tf_op | source)
XLA Modules:
  0.0 32.5 jit_solution(17851330433326854263)
XLA Ops:
  0.6 31.2 %layer.1 = (bf16[256,256]{1,0:T(8,128)(2,1)S(1)}, f32[3,256]{1,0:T(4,128)S(1)}, f32[6,256]{1,0:T(8,128)S(1)}, f32[32,64]{1,0:T(8,128)S(1)}) custom-call(bf16[256,256]{1,0:T(8,128)(2,1)} %refs_0_.1, f32[3,256]{1,0:T(4,128)} %refs_1_.1, s32[4,128]{1,0:T(4,128)} %refs_2_.1, bf16[8,256,256]{2,1,0:T(8,128)(2,1)} %refs_3_.1, bf16[256,256]{1,0:T(8,128)(2,1)} %refs_4_.1, ...), custom_call_target="tpu_custom_call" | custom-call | tf_op jit(solution)/shard_map/layer/pallas_call | solution.py:509
  31.8 0.7 %copy_out.1 = (bf16[256,256]{1,0:T(8,128)(2,1)}, f32[3,256]{1,0:T(4,128)}, f32[6,256]{1,0:T(8,128)}, f32[32,64]{1,0:T(8,128)}) custom-call(bf16[256,256]{1,0:T(8,128)(2,1)S(1)} %get-tuple-element.8.a, f32[3,256]{1,0:T(4,128)S(1)} %get-tuple-element.9.b, f32[6,256]{1,0:T(8,128)S(1)} %get-tuple-element.10.c, f32[32,64]{1,0:T(8,128)S(1)} %get-tuple-element.11.d), custom_call_target="tpu_custom_call" | custom-call | tf_op jit(solution)/shard_map/copy_out/pallas_call | solution.py:521

commit v8 on v7

--- a/solution.py
+++ b/solution.py
@@ -13,7 +13,7 @@
 CELL = 2.0
 GROUP = 4
 WIDE_GROUP = 48
-BACK_GROUP = 12
+BACK_GROUP = 24
 LOG2E = 1.4426950408889634
 F32 = jnp.float32
 BF16 = jnp.bfloat16
@@ -272,22 +272,53 @@
         take(m.msg_in.at[q], m.near_sem.at[q])
         m.chip[q] = (value[q] + m.msg_in[q].astype(F32)).astype(BF16)
         push(m.chip.at[q], m.chip_in.at[q], m.r_chip.at[q], at(d, across))
+    def twin(near):
+        return pltpu.make_async_remote_copy(
+            m.chip.at[1], m.twin.at[1 - near], m.sent, m.near_sem.at[5] if near else m.r_chip.at[2],
+            device_id=at(d, partner if near else cross), device_id_type=MESH)
+
+    @pl.when(c == 0)
+    def _():
+        twin(0).start()
+        twin(1).start()
+
     for t in range(4):
         columns(own + t)
         table(own + t)
     lax.fori_loop(0, pairs // GROUP, transposed, 0)
+    def activate(one, two):
+        low = (one.astype(F32) + two.astype(F32)).astype(BF16)
+        mixed = mm(low, m.mixing[...])
+        sig = jax.nn.sigmoid(mixed)
+        return low, (m.readout[...] * sig * (1.0 + mixed * (1.0 - sig))).astype(BF16)
+
+    def slope_copy(q):
+        return pltpu.make_async_remote_copy(m.slope.at[c, q], m.slope.at[c, q], m.sent, m.near_sem.at[3],
+                                            device_id=at(d, partner), device_id_type=MESH)
+
     for q in range(2):
         take(m.chip_in.at[q], m.r_chip.at[q])
-        low = (m.chip[q].astype(F32) + m.chip_in[q].astype(F32)).astype(BF16)
-        mixed = mm(low, m.mixing[...])
-        sig = jax.nn.sigmoid(mixed)
-        slope = (m.readout[...] * sig * (1.0 + mixed * (1.0 - sig))).astype(BF16)
+        low, slope = activate(m.chip[q], m.chip_in[q])
         m.slope[c, q] = slope
-        push(m.slope.at[c, q], m.slope.at[c, q], m.near_sem.at[3], at(d, partner))
         m.packed[c, q] = low
+        if q == 0:
+            slope_copy(q).start()
+        else:
+            @pl.when(c == 1)
+            def _():
+                slope_copy(q).start()
     push(m.packed.at[c], m.packed.at[c], m.near_sem.at[4], at(d, partner))
 
-    take(m.slope.at[mate], m.near_sem.at[3])
+    @pl.when(c == 0)
+    def _():
+        take(m.slope.at[mate], m.near_sem.at[3])
+
+    @pl.when(c == 1)
+    def _():
+        take(m.slope.at[mate, 0], m.near_sem.at[3])
+        take(m.twin.at[0], m.near_sem.at[5])
+        take(m.twin.at[1], m.r_chip.at[2])
+        m.slope[mate, 1] = activate(m.twin[0], m.twin[1])[1]
     slope = m.slope[...].reshape(atoms, channels)
     for k in range(kinds):
         wide = nt(slope, m.radmix[k]).astype(BF16)
@@ -372,7 +403,7 @@
         for slot, j in group:
             push(m.gfeat.at[j], m.gp.at[slot], m.near_sem.at[slot], at(d, partner))
     settle(held)
-    lax.fori_loop(0, 2 - 2 * c, backward, 0)
+    lax.fori_loop(0, 1 - c, backward, 0)
     pl.semaphore_wait(m.passed, n_rep - 1)
     for place, (slot, j) in enumerate(held):
         take(m.gp.at[slot], m.near_sem.at[slot])
@@ -384,7 +415,7 @@
     for q in (across, cross, partner):
         push(m.sb.at[0, q], m.ro.at[r], m.r_ro, at(d, q))
     m.ro[r] = m.sb[0, r]
-    lax.fori_loop(2 - 2 * c, pairs // BACK_GROUP, backward, 0)
+    lax.fori_loop(1 - c, pairs // BACK_GROUP, backward, 0)
     for t, o in enumerate(OFFSETS):
         m.side[t] = m.far[sum_at(3, own + t)].astype(BF16)
         push(m.side.at[t], m.rs.at[t], m.r_rs, at(dom_at(-o), r))
@@ -437,8 +468,18 @@
     take(m.part.at[pl.ds(2 * (1 - y), 2), low], m.r_chip.at[1])
     take(m.part.at[cross, high], m.near_sem.at[4])
     finish(1 - y)
-    for copy in started:
+    for copy in started + [slope_copy(0)]:
         copy.wait_send()
+
+    @pl.when(c == 0)
+    def _():
+        twin(0).wait_send()
+        twin(1).wait_send()
+
+    @pl.when(c == 1)
+    def _():
+        slope_copy(1).wait_send()
+
     lax.fori_loop(1, n_dom, lambda i, _: (mix_copy(i).wait_send(), 0)[1], 0)
 
 
@@ -486,7 +527,7 @@
         "carry": pltpu.VMEM((TILE, channels), F32), "far": pltpu.VMEM((pairs + 1, 16, TILE), F32),
         "near": pltpu.VMEM((own, 16, TILE), F32),
         "msg": pltpu.VMEM((2, TILE // 2, channels), BF16), "msg_in": pltpu.VMEM((2, TILE // 2, channels), BF16),
-        "chip": pltpu.VMEM((2, TILE // 2, channels), BF16), "chip_in": pltpu.VMEM((2, TILE // 2, channels), BF16),
+        "chip": pltpu.VMEM((2, TILE // 2, channels), BF16), "twin": pltpu.VMEM((2, TILE // 2, channels), BF16), "chip_in": pltpu.VMEM((2, TILE // 2, channels), BF16),
         "slope": pltpu.VMEM((own, 2, TILE // 2, channels), BF16),
         "packed": pltpu.VMEM((own, 2, TILE // 2, channels), BF16), "radmix": pltpu.VMEM(radial.shape, BF16),
         "weights": pltpu.VMEM((own * kinds, TILE, channels), BF16),
@@ -499,7 +540,7 @@
         "eye": pltpu.VMEM((max(atoms, channels),) * 2, BF16),
         "pside": pltpu.VMEM((n_rep, 16, atoms), BF16),
         "load": dma((3,)), "sent": dma, "passed": pltpu.SemaphoreType.REGULAR, "r_pos": dma,
-        "r_feat": dma((2, 2)), "near_sem": dma((5,)), "r_chip": dma((2,)),
+        "r_feat": dma((2, 2)), "near_sem": dma((6,)), "r_chip": dma((3,)),
         "r_rf": dma((2,)), "r_ro": dma, "r_rs": dma, "r_mix": dma,
     }
 

time: 32.7 us -> 32.6 us (level)
  no operation moved by 1% of the time
where the time goes in v8:
time: 32.6 us; the launch traced here: 32.5 us
  Pallas kernels  31.8 us (98%)
  between operations  0.64 us (2%)
    pallas_call x1, Pallas kernels, on_device(): pl.pallas_call(functools.partial(kernel, INPUTS + OUTPUTS + tuple(scratch...  31.2 us
    pallas_call x1, Pallas kernels, on_device(): pl.pallas_call(copy_out, out_shape=tuple((shape(a.shape, a.dtype) for a i...  0.67 us

profile of v8, /device:TPU:0, one launch (start us, length us, event | category | flops | bytes accessed | tf_op | source)
XLA Modules:
  0.0 32.5 jit_solution(6632890928872591227)
XLA Ops:
  0.6 31.2 %layer.1 = (bf16[256,256]{1,0:T(8,128)(2,1)S(1)}, f32[3,256]{1,0:T(4,128)S(1)}, f32[6,256]{1,0:T(8,128)S(1)}, f32[32,64]{1,0:T(8,128)S(1)}) custom-call(bf16[256,256]{1,0:T(8,128)(2,1)} %refs_0_.1, f32[3,256]{1,0:T(4,128)} %refs_1_.1, s32[4,128]{1,0:T(4,128)} %refs_2_.1, bf16[8,256,256]{2,1,0:T(8,128)(2,1)} %refs_3_.1, bf16[256,256]{1,0:T(8,128)(2,1)} %refs_4_.1, ...), custom_call_target="tpu_custom_call" | custom-call | tf_op jit(solution)/shard_map/layer/pallas_call | solution.py:550
  31.8 0.7 %copy_out.1 = (bf16[256,256]{1,0:T(8,128)(2,1)}, f32[3,256]{1,0:T(4,128)}, f32[6,256]{1,0:T(8,128)}, f32[32,64]{1,0:T(8,128)}) custom-call(bf16[256,256]{1,0:T(8,128)(2,1)S(1)} %get-tuple-element.8.a, f32[3,256]{1,0:T(4,128)S(1)} %get-tuple-element.9.b, f32[6,256]{1,0:T(8,128)S(1)} %get-tuple-element.10.c, f32[32,64]{1,0:T(8,128)S(1)} %get-tuple-element.11.d), custom_call_target="tpu_custom_call" | custom-call | tf_op jit(solution)/shard_map/copy_out/pallas_call | solution.py:562

commit v9 on v8

--- a/solution.py
+++ b/solution.py
@@ -11,9 +11,7 @@
 TILE = 128
 OFFSETS = (1, -1, 2, -2)
 CELL = 2.0
-GROUP = 4
-WIDE_GROUP = 48
-BACK_GROUP = 24
+GROUP = 8
 LOG2E = 1.4426950408889634
 F32 = jnp.float32
 BF16 = jnp.bfloat16
@@ -71,6 +69,7 @@
     own = atoms // TILE
     late = lax.div(n_dom - 1 - d, n_dom // 2)
     pairs = m.home.shape[0]
+    back_group = pairs // 2
     kinds = m.radial.shape[0]
     n_ext = m.tiles.shape[0]
     size = TILE // 2
@@ -185,7 +184,6 @@
     for q in peers:
         pl.semaphore_signal(m.passed, inc=1, device_id=at(d, q), device_id_type=MESH)
     m.sums[0] = jnp.zeros_like(m.sums[0])
-    m.carry[...] = jnp.zeros_like(m.carry)
     for t in range(4):
         m.hot[t % 2, :, t // 2 * TILE:(t // 2 + 1) * TILE] = (iota == m.rows[t:t + 1, :]).astype(F32).astype(BF16)
     m.far[0] = jnp.zeros_like(m.far[0])
@@ -246,19 +244,15 @@
     def seg_f(p):
         return m.home[p] * kinds + m.kind[p]
 
-    def forward(g, _):
-        acc = m.carry[...]
-        for u in range(WIDE_GROUP):
-            i = g * WIDE_GROUP + u
+    def forward():
+        acc = None
+        for i in range(pairs):
             p = pair_at(0, i)
-            last = pair_at(0, jnp.maximum(i - 1, 0))
-            keep = (seg_f(p) == seg_f(last)).astype(F32)
-            acc = acc * keep + mm(m.kern_ab[p], m.ext[m.other[p]])
+            part = mm(m.kern_ab[p], m.ext[m.other[p]])
+            acc = part if i == 0 else acc * (seg_f(p) == seg_f(pair_at(0, i - 1))).astype(F32) + part
             m.sums[i + 1] = acc.astype(BF16)
-        m.carry[...] = acc
-        return 0
-
-    lax.fori_loop(0, pairs // WIDE_GROUP, forward, 0)
+
+    forward()
 
     def message(h):
         left = [m.sums[sum_at(2, h * kinds + k)] for k in range(kinds)]
@@ -344,24 +338,22 @@
         keep = (m.other[p] == m.other[last]).astype(F32)
         return p, m.home[p], m.other[p], m.kind[p], keep
 
-    def spread_back(g, _):
-        acc = m.carry[...]
-        for u in range(WIDE_GROUP):
-            i = g * WIDE_GROUP + u
+    def spread_back():
+        acc = None
+        for i in range(pairs):
             p, h, _, k, keep = pair_b(i)
-            acc = acc * keep + mm(m.kern_ba[p].astype(BF16), m.weights[h * kinds + k])
+            part = mm(m.kern_ba[p].astype(BF16), m.weights[h * kinds + k])
+            acc = part if i == 0 else acc * keep + part
             m.sums[i + 1] = acc.astype(BF16)
-        m.carry[...] = acc
-        return 0
 
     def backward(g, _):
         found = []
-        for u in range(BACK_GROUP):
-            i = g * BACK_GROUP + u
+        for u in range(back_group):
+            i = g * back_group + u
             p, h, o, k, keep = pair_b(i)
             grad = nt(m.ext[o], m.weights[h * kinds + k])
             found.append((i, p, h, o, keep, ((-2.0 * m.decay[k]) * m.kern_ba[p] * grad).astype(BF16)))
-        far = m.far[g * BACK_GROUP]
+        far = m.far[g * back_group]
         near = [m.near[j] for j in range(own)]
         results = []
         for one, two in zip(found[::2], found[1::2]):
@@ -384,8 +376,7 @@
             m.near[j] = near[j]
         return 0
 
-    m.carry[...] = jnp.zeros_like(m.carry)
-    lax.fori_loop(0, pairs // WIDE_GROUP, spread_back, 0)
+    spread_back()
 
     share = channels // n_rep
     slots = (2 - late, 1 + late, 0)
@@ -415,7 +406,7 @@
     for q in (across, cross, partner):
         push(m.sb.at[0, q], m.ro.at[r], m.r_ro, at(d, q))
     m.ro[r] = m.sb[0, r]
-    lax.fori_loop(1 - c, pairs // BACK_GROUP, backward, 0)
+    lax.fori_loop(1 - c, pairs // back_group, backward, 0)
     for t, o in enumerate(OFFSETS):
         m.side[t] = m.far[sum_at(3, own + t)].astype(BF16)
         push(m.side.at[t], m.rs.at[t], m.r_rs, at(dom_at(-o), r))
@@ -439,7 +430,7 @@
 
     total = total + gather(1 - late)
     m.part[r] = (total + gather(late)).astype(BF16)
-    low, high = pl.ds(0, share - share // 4), pl.ds(share - share // 4, share // 4)
+    low, high = pl.ds(0, share // 2), pl.ds(share // 2, share // 2)
     push(m.part.at[r, high], m.part.at[r, high], m.r_chip.at[0], at(d, across))
     push(m.part.at[r, low], m.part.at[r, low], m.r_chip.at[1], at(d, across))
     push(m.part.at[r, low], m.part.at[r, low], m.r_chip.at[1], at(d, cross))
@@ -523,8 +514,7 @@
         "sided": pltpu.VMEM((own, 2, 80, 2 * TILE), BF16), "hot": pltpu.VMEM((2, atoms, 2 * TILE), BF16),
         "first": pltpu.VMEM((n_ext, 8, TILE), F32), "second": pltpu.VMEM((n_ext, 8, TILE), F32),
         "kern_ab": pltpu.VMEM((pairs, TILE, TILE), BF16), "kern_ba": pltpu.VMEM((pairs, TILE, TILE), F32),
-        "sums": pltpu.VMEM((pairs + 1, TILE, channels), BF16),
-        "carry": pltpu.VMEM((TILE, channels), F32), "far": pltpu.VMEM((pairs + 1, 16, TILE), F32),
+        "sums": pltpu.VMEM((pairs + 1, TILE, channels), BF16), "far": pltpu.VMEM((pairs + 1, 16, TILE), F32),
         "near": pltpu.VMEM((own, 16, TILE), F32),
         "msg": pltpu.VMEM((2, TILE // 2, channels), BF16), "msg_in": pltpu.VMEM((2, TILE // 2, channels), BF16),
         "chip": pltpu.VMEM((2, TILE // 2, channels), BF16), "twin": pltpu.VMEM((2, TILE // 2, channels), BF16), "chip_in": pltpu.VMEM((2, TILE // 2, channels), BF16),

time: 32.6 us -> 32.7 us (level)
  no operation moved by 1% of the time
where the time goes in v9:
time: 32.7 us; the launch traced here: 32.4 us
  Pallas kernels  31.8 us (97%)
  between operations  0.64 us (2%)
    pallas_call x1, Pallas kernels, on_device(): pl.pallas_call(functools.partial(kernel, INPUTS + OUTPUTS + tuple(scratch...  31.1 us
    pallas_call x1, Pallas kernels, on_device(): pl.pallas_call(copy_out, out_shape=tuple((shape(a.shape, a.dtype) for a i...  0.67 us

profile of v9, /device:TPU:0, one launch (start us, length us, event | category | flops | bytes accessed | tf_op | source)
XLA Modules:
  0.0 32.4 jit_solution(13040626027244680762)
XLA Ops:
  0.6 31.1 %layer.1 = (bf16[256,256]{1,0:T(8,128)(2,1)S(1)}, f32[3,256]{1,0:T(4,128)S(1)}, f32[6,256]{1,0:T(8,128)S(1)}, f32[32,64]{1,0:T(8,128)S(1)}) custom-call(bf16[256,256]{1,0:T(8,128)(2,1)} %refs_0_.1, f32[3,256]{1,0:T(4,128)} %refs_1_.1, s32[4,128]{1,0:T(4,128)} %refs_2_.1, bf16[8,256,256]{2,1,0:T(8,128)(2,1)} %refs_3_.1, bf16[256,256]{1,0:T(8,128)(2,1)} %refs_4_.1, ...), custom_call_target="tpu_custom_call" | custom-call | tf_op jit(solution)/shard_map/layer/pallas_call | solution.py:540
  31.7 0.7 %copy_out.1 = (bf16[256,256]{1,0:T(8,128)(2,1)}, f32[3,256]{1,0:T(4,128)}, f32[6,256]{1,0:T(8,128)}, f32[32,64]{1,0:T(8,128)}) custom-call(bf16[256,256]{1,0:T(8,128)(2,1)S(1)} %get-tuple-element.8.a, f32[3,256]{1,0:T(4,128)S(1)} %get-tuple-element.9.b, f32[6,256]{1,0:T(8,128)S(1)} %get-tuple-element.10.c, f32[32,64]{1,0:T(8,128)S(1)} %get-tuple-element.11.d), custom_call_target="tpu_custom_call" | custom-call | tf_op jit(solution)/shard_map/copy_out/pallas_call | solution.py:552

commit v10 on v8

--- a/solution.py
+++ b/solution.py
@@ -11,7 +11,7 @@
 TILE = 128
 OFFSETS = (1, -1, 2, -2)
 CELL = 2.0
-GROUP = 4
+GROUP = 12
 WIDE_GROUP = 48
 BACK_GROUP = 24
 LOG2E = 1.4426950408889634

time: 32.6 us -> 32.6 us (level)
  no operation moved by 1% of the time
where the time goes in v10:
time: 32.6 us; the launch traced here: 32.5 us
  Pallas kernels  31.8 us (98%)
  between operations  0.64 us (2%)
    pallas_call x1, Pallas kernels, on_device(): pl.pallas_call(functools.partial(kernel, INPUTS + OUTPUTS + tuple(scratch...  31.2 us
    pallas_call x1, Pallas kernels, on_device(): pl.pallas_call(copy_out, out_shape=tuple((shape(a.shape, a.dtype) for a i...  0.67 us

profile of v10, /device:TPU:0, one launch (start us, length us, event | category | flops | bytes accessed | tf_op | source)
XLA Modules:
  0.0 32.5 jit_solution(16393413438745927899)
XLA Ops:
  0.6 31.2 %layer.1 = (bf16[256,256]{1,0:T(8,128)(2,1)S(1)}, f32[3,256]{1,0:T(4,128)S(1)}, f32[6,256]{1,0:T(8,128)S(1)}, f32[32,64]{1,0:T(8,128)S(1)}) custom-call(bf16[256,256]{1,0:T(8,128)(2,1)} %refs_0_.1, f32[3,256]{1,0:T(4,128)} %refs_1_.1, s32[4,128]{1,0:T(4,128)} %refs_2_.1, bf16[8,256,256]{2,1,0:T(8,128)(2,1)} %refs_3_.1, bf16[256,256]{1,0:T(8,128)(2,1)} %refs_4_.1, ...), custom_call_target="tpu_custom_call" | custom-call | tf_op jit(solution)/shard_map/layer/pallas_call | solution.py:550
  31.8 0.7 %copy_out.1 = (bf16[256,256]{1,0:T(8,128)(2,1)}, f32[3,256]{1,0:T(4,128)}, f32[6,256]{1,0:T(8,128)}, f32[32,64]{1,0:T(8,128)}) custom-call(bf16[256,256]{1,0:T(8,128)(2,1)S(1)} %get-tuple-element.8.a, f32[3,256]{1,0:T(4,128)S(1)} %get-tuple-element.9.b, f32[6,256]{1,0:T(8,128)S(1)} %get-tuple-element.10.c, f32[32,64]{1,0:T(8,128)S(1)} %get-tuple-element.11.d), custom_call_target="tpu_custom_call" | custom-call | tf_op jit(solution)/shard_map/copy_out/pallas_call | solution.py:562
